TPU v7x, 32 devices: a whole 2x2x4 slice. The times are simulated.
32 devices in a mesh: ctx: 4 (over x, core), fsdp: 8 (over z, y).
Axes of the slice: x: 2, y: 2, z: 4, core: 2. Of those that a mesh axis runs over, the one named last changes fastest.
Arguments:
- inputs: bfloat16 [2, 8, 512, 1024], P(None, 'fsdp', 'ctx'), may hold values from -6 to 6
- cotangent: bfloat16 [2, 8, 512, 1024], P(None, 'fsdp', 'ctx'), may hold values from -6 to 6
- lengths: int32 [2, 8], P(None, 'fsdp'), may hold values from 128 to 512, as said below
- query_weight: bfloat16 [1024, 1024], P('fsdp'), may hold values from -0.1875 to 0.1875
- key_weight: bfloat16 [1024, 1024], P('fsdp'), may hold values from -0.1875 to 0.1875
- value_weight: bfloat16 [1024, 1024], P('fsdp'), may hold values from -0.1875 to 0.1875
- output_weight: bfloat16 [1024, 1024], P('fsdp'), may hold values from -0.75 to 0.75
- query_bias: bfloat16 [1024], P('fsdp'), may hold values from -3 to 3
- value_bias: bfloat16 [1024], P('fsdp'), may hold values from -3 to 3
- output_bias: bfloat16 [1024], P('fsdp'), may hold values from -2 to 2
- first_gain: bfloat16 [1024], P('fsdp'), may hold values from 0.099609375 to 1.8984375
- first_shift: bfloat16 [1024], P('fsdp'), may hold values from -2 to 2
- inner_weight: bfloat16 [1024, 4096], P('fsdp'), may hold values from -0.1875 to 0.1875
- inner_bias: bfloat16 [4096], P('fsdp'), may hold values from -3 to 3
- outer_weight: bfloat16 [4096, 1024], P('fsdp'), may hold values from -0.09375 to 0.09375
- outer_bias: bfloat16 [1024], P('fsdp'), may hold values from -2 to 2
- second_gain: bfloat16 [1024], P('fsdp'), may hold values from 0.099609375 to 1.8984375
- second_shift: bfloat16 [1024], P('fsdp'), may hold values from -2 to 2
Outputs:
- layer_output: bfloat16 [2, 8, 512, 1024], P(None, 'fsdp', 'ctx')
- input_gradient: float32 [2, 8, 512, 1024], P(None, 'fsdp', 'ctx')
- query_weight_gradient: float32 [1024, 1024], P('fsdp')
- key_weight_gradient: float32 [1024, 1024], P('fsdp')
- value_weight_gradient: float32 [1024, 1024], P('fsdp')
- output_weight_gradient: float32 [1024, 1024], P('fsdp')
- query_bias_gradient: float32 [1024], P('fsdp')
- value_bias_gradient: float32 [1024], P('fsdp')
- output_bias_gradient: float32 [1024], P('fsdp')
- first_gain_gradient: float32 [1024], P('fsdp')
- first_shift_gradient: float32 [1024], P('fsdp')
- inner_weight_gradient: float32 [1024, 4096], P('fsdp')
- inner_bias_gradient: float32 [4096], P('fsdp')
- outer_weight_gradient: float32 [4096, 1024], P('fsdp')
- outer_bias_gradient: float32 [1024], P('fsdp')
- second_gain_gradient: float32 [1024], P('fsdp')
- second_shift_gradient: float32 [1024], P('fsdp')
Inputs may be any that keep to these rules, and one draw needn't show every extreme that they name: The valid slots of a sequence are its first lengths entries; in every micro-batch some sequence fills all 512 slots.
All inputs are finite; a program needn't handle non-finite values.
Results may differ from a plain program's by a relative error of at most 0.018.
Values may be sent and summed in bfloat16 or wider, within the bound.
A program may use at most 256 MiB of HBM per device.

v0:
```python
import jax
import jax.numpy as jnp
from jax import lax
from jax.sharding import PartitionSpec as P

HEAD_DIM = 64


EPSILON = 1e-06


def layer_norm(hidden, gain, shift):
    average = jnp.mean(hidden, axis=-1, keepdims=True)
    centered = hidden - average
    variance = jnp.mean(centered * centered, axis=-1, keepdims=True)
    return centered * lax.rsqrt(variance + EPSILON) * gain + shift


def exact_gelu(hidden):
    return jax.nn.gelu(hidden, approximate=False)


def plain_product(left, right):
    return jnp.dot(left, right, preferred_element_type=jnp.float32)


def left_product(left, right):
    return lax.dot_general(
        left, right, (((0,), (0,)), ((), ())), preferred_element_type=jnp.float32
    )


def right_product(left, right):
    return lax.dot_general(
        left, right, (((1,), (1,)), ((), ())), preferred_element_type=jnp.float32
    )


def column_sums(rows_low):
    return jnp.sum(rows_low.astype(jnp.float32), axis=0)


def reduce_feedforward(parts):
    shares = (
        lax.psum_scatter(parts[0], "fsdp", scatter_dimension=0, tiled=True),
        lax.psum_scatter(parts[1], "fsdp", scatter_dimension=0, tiled=True),
        lax.psum_scatter(parts[2], "fsdp", scatter_dimension=0, tiled=True),
        lax.psum_scatter(parts[3], "fsdp", scatter_dimension=0, tiled=True),
        lax.psum_scatter(parts[4], "fsdp", scatter_dimension=0, tiled=True),
        lax.psum_scatter(parts[5], "fsdp", scatter_dimension=0, tiled=True),
    )
    return (
        lax.psum(shares[0].astype(jnp.bfloat16), "ctx").astype(jnp.float32),
        lax.psum(shares[1].astype(jnp.bfloat16), "ctx").astype(jnp.float32),
        lax.psum(shares[2].astype(jnp.bfloat16), "ctx").astype(jnp.float32),
        lax.psum(shares[3].astype(jnp.bfloat16), "ctx").astype(jnp.float32),
        lax.psum(shares[4].astype(jnp.bfloat16), "ctx").astype(jnp.float32),
        lax.psum(shares[5].astype(jnp.bfloat16), "ctx").astype(jnp.float32),
    )


def reduce_attention(parts):
    shares = (
        lax.psum_scatter(parts[0], "fsdp", scatter_dimension=0, tiled=True),
        lax.psum_scatter(parts[1], "fsdp", scatter_dimension=0, tiled=True),
        lax.psum_scatter(parts[2], "fsdp", scatter_dimension=0, tiled=True),
        lax.psum_scatter(parts[3], "fsdp", scatter_dimension=0, tiled=True),
        lax.psum_scatter(parts[4], "fsdp", scatter_dimension=0, tiled=True),
        lax.psum_scatter(parts[5], "fsdp", scatter_dimension=0, tiled=True),
        lax.psum_scatter(parts[6], "fsdp", scatter_dimension=0, tiled=True),
        lax.psum_scatter(parts[7], "fsdp", scatter_dimension=0, tiled=True),
        lax.psum_scatter(parts[8], "fsdp", scatter_dimension=0, tiled=True),
    )
    return (
        lax.psum(shares[0].astype(jnp.bfloat16), "ctx").astype(jnp.float32),
        lax.psum(shares[1].astype(jnp.bfloat16), "ctx").astype(jnp.float32),
        lax.psum(shares[2].astype(jnp.bfloat16), "ctx").astype(jnp.float32),
        lax.psum(shares[3].astype(jnp.bfloat16), "ctx").astype(jnp.float32),
        lax.psum(shares[4].astype(jnp.bfloat16), "ctx").astype(jnp.float32),
        lax.psum(shares[5].astype(jnp.bfloat16), "ctx").astype(jnp.float32),
        lax.psum(shares[6].astype(jnp.bfloat16), "ctx").astype(jnp.float32),
        lax.psum(shares[7].astype(jnp.bfloat16), "ctx").astype(jnp.float32),
        lax.psum(shares[8].astype(jnp.bfloat16), "ctx").astype(jnp.float32),
    )


def body(
    inputs,
    cotangent,
    lengths,
    query_weight,
    key_weight,
    value_weight,
    output_weight,
    query_bias,
    value_bias,
    output_bias,
    first_gain,
    first_shift,
    inner_weight,
    inner_bias,
    outer_weight,
    outer_bias,
    second_gain,
    second_shift,
):
    (
        full_query,
        full_key,
        full_value,
        full_output,
        bias_query,
        bias_value,
        bias_output,
        gain_first,
        shift_first,
    ) = (
        lax.all_gather(query_weight, "fsdp", axis=0, tiled=True),
        lax.all_gather(key_weight, "fsdp", axis=0, tiled=True),
        lax.all_gather(value_weight, "fsdp", axis=0, tiled=True),
        lax.all_gather(output_weight, "fsdp", axis=0, tiled=True),
        lax.all_gather(query_bias, "fsdp", axis=0, tiled=True),
        lax.all_gather(value_bias, "fsdp", axis=0, tiled=True),
        lax.all_gather(output_bias, "fsdp", axis=0, tiled=True),
        lax.all_gather(first_gain, "fsdp", axis=0, tiled=True),
        lax.all_gather(first_shift, "fsdp", axis=0, tiled=True),
    )
    full_inner, bias_inner, full_outer, bias_outer, gain_second, shift_second = (
        lax.all_gather(inner_weight, "fsdp", axis=0, tiled=True),
        lax.all_gather(inner_bias, "fsdp", axis=0, tiled=True),
        lax.all_gather(outer_weight, "fsdp", axis=0, tiled=True),
        lax.all_gather(outer_bias, "fsdp", axis=0, tiled=True),
        lax.all_gather(second_gain, "fsdp", axis=0, tiled=True),
        lax.all_gather(second_shift, "fsdp", axis=0, tiled=True),
    )
    bias_query = bias_query.astype(jnp.float32)
    bias_value = bias_value.astype(jnp.float32)
    bias_output = bias_output.astype(jnp.float32)
    gain_first = gain_first.astype(jnp.float32)
    shift_first = shift_first.astype(jnp.float32)
    bias_inner = bias_inner.astype(jnp.float32)
    bias_outer = bias_outer.astype(jnp.float32)
    gain_second = gain_second.astype(jnp.float32)
    shift_second = shift_second.astype(jnp.float32)
    micro_count, seq_count, block_len, model_width = inputs.shape
    heads = model_width // HEAD_DIM
    total_slots = block_len * lax.axis_size("ctx")
    local_pos = lax.axis_index("ctx") * block_len + jnp.arange(block_len, dtype=jnp.int32)
    global_pos = jnp.arange(total_slots, dtype=jnp.int32)
    scale = HEAD_DIM ** (-0.5)
    row_count = seq_count * block_len

    def one_batch(totals, pieces):
        batch_in, batch_ct, batch_len = pieces
        flat_rows = batch_in.reshape(row_count, model_width)
        own_valid = local_pos[None, :] < batch_len[:, None]
        row_mask = own_valid.astype(jnp.float32).reshape(row_count, 1)
        key_valid = global_pos[None, :] < batch_len[:, None]
        queries = (plain_product(flat_rows, full_query) + bias_query).astype(jnp.bfloat16)
        keys_here = plain_product(flat_rows, full_key).astype(jnp.bfloat16)
        values_here = (plain_product(flat_rows, full_value) + bias_value).astype(jnp.bfloat16)
        keys_all, values_all = (
            lax.all_gather(
                keys_here.reshape(seq_count, block_len, model_width), "ctx", axis=1, tiled=True
            ),
            lax.all_gather(
                values_here.reshape(seq_count, block_len, model_width), "ctx", axis=1, tiled=True
            ),
        )
        query_heads = queries.reshape(seq_count, block_len, heads, HEAD_DIM)
        key_heads = keys_all.reshape(seq_count, total_slots, heads, HEAD_DIM)
        value_heads = values_all.reshape(seq_count, total_slots, heads, HEAD_DIM)

        def score_block():
            raw_scores = (
                jnp.einsum(
                    "sqhd,skhd->shqk", query_heads, key_heads, preferred_element_type=jnp.float32
                )
                * scale
            )
            return jnp.where(key_valid[:, None, None, :], raw_scores, -1e30)

        scores = score_block()
        top_score = jnp.max(scores, axis=-1, keepdims=True)
        log_total = top_score + jnp.log(
            jnp.sum(jnp.exp(scores - top_score), axis=-1, keepdims=True)
        )
        probs_low = jnp.exp(scores - log_total).astype(jnp.bfloat16)
        context = jnp.einsum(
            "shqk,skhd->sqhd", probs_low, value_heads, preferred_element_type=jnp.float32
        )
        context = context.reshape(row_count, model_width).astype(jnp.bfloat16)
        first_sum = (
            flat_rows.astype(jnp.float32) + plain_product(context, full_output) + bias_output
        )
        normed, first_back = jax.vjp(layer_norm, first_sum, gain_first, shift_first)
        normed_low = normed.astype(jnp.bfloat16)
        hidden = plain_product(normed_low, full_inner) + bias_inner
        active, gelu_back = jax.vjp(exact_gelu, hidden)
        active_low = active.astype(jnp.bfloat16)
        second_sum = normed + plain_product(active_low, full_outer) + bias_outer
        final_rows, second_back = jax.vjp(layer_norm, second_sum, gain_second, shift_second)
        output = (
            (final_rows * row_mask).astype(jnp.bfloat16).reshape(seq_count, block_len, model_width)
        )
        out_grad = batch_ct.reshape(row_count, model_width).astype(jnp.float32) * row_mask
        second_grad, second_gain_part, second_shift_part = second_back(out_grad)
        second_low = second_grad.astype(jnp.bfloat16)
        outer_weight_part = left_product(active_low, second_low)
        outer_bias_part = column_sums(second_low)
        (hidden_grad,) = gelu_back(right_product(second_low, full_outer))
        hidden_low = hidden_grad.astype(jnp.bfloat16)
        inner_weight_part = left_product(normed_low, hidden_low)
        inner_bias_part = column_sums(hidden_low)
        normed_grad = second_grad + right_product(hidden_low, full_inner)
        first_grad, first_gain_part, first_shift_part = first_back(normed_grad)
        branch_low = first_grad.astype(jnp.bfloat16)
        output_weight_part = left_product(context, branch_low)
        output_bias_part = column_sums(branch_low)
        context_flat = right_product(branch_low, full_output).astype(jnp.bfloat16)
        context_grad = context_flat.reshape(seq_count, block_len, heads, HEAD_DIM)
        probs_again = jnp.exp(score_block() - log_total)
        probs_grad = jnp.einsum(
            "sqhd,skhd->shqk", context_grad, value_heads, preferred_element_type=jnp.float32
        )
        inner_total = jnp.sum(probs_again * probs_grad, axis=-1, keepdims=True)
        scores_grad = (probs_again * (probs_grad - inner_total)).astype(jnp.bfloat16)
        query_grad = jnp.einsum(
            "shqk,skhd->sqhd", scores_grad, key_heads, preferred_element_type=jnp.float32
        )
        query_grad = (query_grad * scale).astype(jnp.bfloat16).reshape(row_count, model_width)
        key_part = (
            jnp.einsum(
                "shqk,sqhd->skhd", scores_grad, query_heads, preferred_element_type=jnp.float32
            )
            * scale
        )
        value_part = jnp.einsum(
            "shqk,sqhd->skhd",
            probs_again.astype(jnp.bfloat16),
            context_grad,
            preferred_element_type=jnp.float32,
        )
        key_grad, value_grad = (
            lax.psum_scatter(
                key_part.reshape(seq_count, total_slots, model_width).astype(jnp.bfloat16),
                "ctx",
                scatter_dimension=1,
                tiled=True,
            ).astype(jnp.float32),
            lax.psum_scatter(
                value_part.reshape(seq_count, total_slots, model_width).astype(jnp.bfloat16),
                "ctx",
                scatter_dimension=1,
                tiled=True,
            ).astype(jnp.float32),
        )
        key_low = key_grad.astype(jnp.bfloat16).reshape(row_count, model_width)
        value_low = value_grad.astype(jnp.bfloat16).reshape(row_count, model_width)
        query_weight_part = left_product(flat_rows, query_grad)
        query_bias_part = column_sums(query_grad)
        key_weight_part = left_product(flat_rows, key_low)
        value_weight_part = left_product(flat_rows, value_low)
        value_bias_part = column_sums(value_low)
        input_grad = (
            first_grad
            + right_product(query_grad, full_query)
            + right_product(key_low, full_key)
            + right_product(value_low, full_value)
        )
        additions = (
            query_weight_part,
            key_weight_part,
            value_weight_part,
            output_weight_part,
            query_bias_part,
            value_bias_part,
            output_bias_part,
            first_gain_part,
            first_shift_part,
            inner_weight_part,
            inner_bias_part,
            outer_weight_part,
            outer_bias_part,
            second_gain_part,
            second_shift_part,
        )
        new_totals = tuple((running + extra for running, extra in zip(totals, additions)))
        return (new_totals, (output, input_grad.reshape(seq_count, block_len, model_width)))

    gathered = (
        full_query,
        full_key,
        full_value,
        full_output,
        bias_query,
        bias_value,
        bias_output,
        gain_first,
        shift_first,
        full_inner,
        bias_inner,
        full_outer,
        bias_outer,
        gain_second,
        shift_second,
    )
    zero_grads = tuple((jnp.zeros(member.shape, jnp.float32) for member in gathered))
    totals, (outputs, input_grads) = lax.scan(one_batch, zero_grads, (inputs, cotangent, lengths))
    feedforward = reduce_feedforward(totals[9:15])
    attention = reduce_attention(totals[0:9])
    return (
        outputs,
        input_grads,
        attention[0],
        attention[1],
        attention[2],
        attention[3],
        attention[4],
        attention[5],
        attention[6],
        attention[7],
        attention[8],
        feedforward[0],
        feedforward[1],
        feedforward[2],
        feedforward[3],
        feedforward[4],
        feedforward[5],
    )


def solution(mesh):
    return jax.shard_map(
        body,
        mesh=mesh,
        in_specs=(
            P(None, "fsdp", "ctx", None),
            P(None, "fsdp", "ctx", None),
            P(None, "fsdp"),
            P("fsdp", None),
            P("fsdp", None),
            P("fsdp", None),
            P("fsdp", None),
            P("fsdp"),
            P("fsdp"),
            P("fsdp"),
            P("fsdp"),
            P("fsdp"),
            P("fsdp", None),
            P("fsdp"),
            P("fsdp", None),
            P("fsdp"),
            P("fsdp"),
            P("fsdp"),
        ),
        out_specs=(
            P(None, "fsdp", "ctx", None),
            P(None, "fsdp", "ctx", None),
            P("fsdp", None),
            P("fsdp", None),
            P("fsdp", None),
            P("fsdp", None),
            P("fsdp"),
            P("fsdp"),
            P("fsdp"),
            P("fsdp"),
            P("fsdp"),
            P("fsdp", None),
            P("fsdp"),
            P("fsdp", None),
            P("fsdp"),
            P("fsdp"),
            P("fsdp"),
        ),
        check_vma=False,
    )
```

profile of v0, /device:TPU:1, one launch (start us, length us, event | category | flops | bytes accessed | tf_op | source)
XLA Modules:
  0.0 1796.3 jit_solution(8527903402704886772)
XLA Ops:
  11.5 23.6 %all-gather.8 = bf16[8,1,512]{2,1,0:T(2,128)(2,1)S(1)} all-gather(bf16[1,1,512]{2,1,0:T(2,128)(2,1)S(1)} %reshape.283), channel_id=1, replica_groups=mesh['ctx'=4,'fsdp'=8] {'fsdp'}, dimensions={0}, use_global_device_ids=true | all-gather | bytes 9216 | tf_op jit(solution)/shard_map/all_gather | solution.py:130
  35.1 15.4 all-gather.2
  50.5 12.9 all-gather.7
  63.4 14.5 all-gather.9
  77.9 12.7 all-gather.10
  90.7 14.6 all-gather.3
  105.3 13.2 all-gather.4
  118.5 13.9 all-gather.5
  132.4 13.9 all-gather.6
  146.3 14.4 all-gather.30.cloned.1.call-done
  160.7 49.8 %all-gather.32.cloned.1.call-done = bf16[1024,1024]{1,0:T(8,128)(2,1)} async-done(((bf16[128,1024]{1,0:T(8,128)(2,1)}), bf16[1024,1024]{1,0:T(8,128)(2,1)}) %all-gather.32.cloned.1.call-update) | async-done | bytes 2097168 | tf_op jit(solution)/shard_map/all_gather | solution.py:121
  210.5 126.1 %all-gather.34.cloned.1.call-done = bf16[1024,4096]{1,0:T(8,128)(2,1)} async-done(((bf16[128,4096]{1,0:T(8,128)(2,1)}), bf16[1024,4096]{1,0:T(8,128)(2,1)}) %all-gather.34.cloned.1.call-update) | async-done | bytes 8388624 | tf_op jit(solution)/shard_map/all_gather | solution.py:129
  336.7 125.1 %all-gather.36.cloned.1.call-done = bf16[4096,1024]{1,0:T(8,128)(2,1)} async-done(((bf16[512,1024]{1,0:T(8,128)(2,1)}), bf16[4096,1024]{1,0:T(8,128)(2,1)}) %all-gather.36.cloned.1.call-update) | async-done | bytes 8388624 | tf_op jit(solution)/shard_map/all_gather | solution.py:131
  461.8 308.7 %while.43 = (s32[]{:T(128)}, f32[1024,1024]{1,0:T(8,128)}, f32[1024,1024]{1,0:T(8,128)}, f32[1024,1024]{1,0:T(8,128)}, f32[1024,1024]{1,0:T(8,128)}, /*index=5*/...) while((s32[]{:T(128)}, f32[1024,1024]{1,0:T(8,128)}, ...), condition=%wide.region_23.24_spmd.clone, body=%wide.region_0.23_spmd.clone.sunk | while | flops 10578308096 | bytes 465342752 | solution.py:309
  470.2 10.3 all-gather.38.cloned.1.call-done
  485.0 14.4 all-gather.40.cloned.1.call-done
  506.3 9.9 multiply_convert_fusion.7
  581.8 8.2 select_add_fusion.35
  618.1 11.8 all-gather.38.cloned.1.call-done
  634.4 14.3 all-gather.40.cloned.1.call-done
  655.6 9.9 multiply_convert_fusion.7
  726.5 14.2 select_add_fusion.37
  740.7 14.2 select_add_fusion.35
  774.2 87.9 %reduce-scatter.17.cloned.1.call-done = f32[128,1024]{1,0:T(8,128)} async-done(((f32[1024,1024]{1,0:T(8,128)}), f32[128,1024]{1,0:T(8,128)}) %reduce-scatter.17.cloned.1.call-update) | async-done | bytes 524304 | tf_op jit(solution)/shard_map/reduce_scatter | solution.py:64
  863.9 90.0 %reduce-scatter.19.cloned.1.call-done = f32[128,1024]{1,0:T(8,128)} async-done(((f32[1024,1024]{1,0:T(8,128)}), f32[128,1024]{1,0:T(8,128)}) %reduce-scatter.19.cloned.1.call-update) | async-done | bytes 524304 | tf_op jit(solution)/shard_map/reduce_scatter | solution.py:65
  955.7 89.6 %reduce-scatter.21.cloned.1.call-done = f32[128,1024]{1,0:T(8,128)} async-done(((f32[1024,1024]{1,0:T(8,128)}), f32[128,1024]{1,0:T(8,128)}) %reduce-scatter.21.cloned.1.call-update) | async-done | bytes 524304 | tf_op jit(solution)/shard_map/reduce_scatter | solution.py:66
  1047.0 89.8 %reduce-scatter.23.cloned.1.call-done = f32[128,1024]{1,0:T(8,128)} async-done(((f32[1024,1024]{1,0:T(8,128)}), f32[128,1024]{1,0:T(8,128)}) %reduce-scatter.23.cloned.1.call-update) | async-done | bytes 524304 | tf_op jit(solution)/shard_map/reduce_scatter | solution.py:67
  1138.7 284.4 %reduce-scatter.25.cloned.1.call-done = f32[128,4096]{1,0:T(8,128)} async-done(((f32[1024,4096]{1,0:T(8,128)}), f32[128,4096]{1,0:T(8,128)}) %reduce-scatter.25.cloned.1.call-update) | async-done | bytes 2097168 | tf_op jit(solution)/shard_map/reduce_scatter | solution.py:45
  1425.8 283.2 %reduce-scatter.27.cloned.1.call-done = f32[512,1024]{1,0:T(8,128)} async-done(((f32[4096,1024]{1,0:T(8,128)}), f32[512,1024]{1,0:T(8,128)}) %reduce-scatter.27.cloned.1.call-update) | async-done | bytes 2097168 | tf_op jit(solution)/shard_map/reduce_scatter | solution.py:47
  1714.2 28.7 %all-reduce.9 = (bf16[1024]{0:T(1024)(128)(2,1)S(1)}, bf16[1024]{0:T(1024)(128)(2,1)S(1)}, bf16[1024]{0:T(1024)(128)(2,1)S(1)}, bf16[1024]{0:T(1024)(128)(2,1)S(...) all-reduce(f32[1024]{0:T(1024)S(1)} %get-tuple-element.1040, ...), channel_id=10, replica_groups=mesh['ctx'=4,'fsdp'=8] {'fsdp'}, use_global_device_ids=true, to_apply=%region_32.33.clone | all-reduce | flops 12288 | bytes 73728
  1743.6 12.7 all-reduce.10
  1761.1 20.2 %all-reduce.14.cloned.1.call-done = (bf16[128,1024]{1,0:T(8,128)(2,1)}, bf16[128,1024]{1,0:T(8,128)(2,1)}, bf16[128,1024]{1,0:T(8,128)(2,1)}, bf16[128,1024]{1,0...) async-done(((bf16[128,1024]{1,0:T(8,128)(2,1)}, bf16[128,1024]{1,0:T(8,128)(2,1)}, bf16[128,1024]{1,0:T(8,128)(2,1)}, bf16[128,1024]{1,0:T(8,128)(2,1)}, ...) | async-done | bytes 3145744 | tf_op jit(solution)/shard_map/psum | solution.py:75
  (431 shorter events, 232.2 us)
Async XLA Ops:
  7.2 56.2 %copy-start.42 = (bf16[128]{0:T(256)(128)(2,1)S(1)}, bf16[128]{0:T(256)(128)(2,1)}, u32[]{:S(2)}) copy-start(bf16[128]{0:T(256)(128)(2,1)} %param.35) | copy-start | bytes 772
  7.2 70.7 %copy-start.43 = (bf16[128]{0:T(256)(128)(2,1)S(1)}, bf16[128]{0:T(256)(128)(2,1)}, u32[]{:S(2)}) copy-start(bf16[128]{0:T(256)(128)(2,1)} %param.37) | copy-start | bytes 772
  7.2 83.4 %copy-start.44 = (bf16[128]{0:T(256)(128)(2,1)S(1)}, bf16[128]{0:T(256)(128)(2,1)}, u32[]{:S(2)}) copy-start(bf16[128]{0:T(256)(128)(2,1)} %param.36) | copy-start | bytes 772
  7.3 98.1 %copy-start.45 = (bf16[128]{0:T(256)(128)(2,1)S(1)}, bf16[128]{0:T(256)(128)(2,1)}, u32[]{:S(2)}) copy-start(bf16[128]{0:T(256)(128)(2,1)} %param.28) | copy-start | bytes 772
  7.3 111.3 %copy-start.46 = (bf16[128]{0:T(256)(128)(2,1)S(1)}, bf16[128]{0:T(256)(128)(2,1)}, u32[]{:S(2)}) copy-start(bf16[128]{0:T(256)(128)(2,1)} %param.29) | copy-start | bytes 772
  7.3 125.2 %copy-start.47 = (bf16[128]{0:T(256)(128)(2,1)S(1)}, bf16[128]{0:T(256)(128)(2,1)}, u32[]{:S(2)}) copy-start(bf16[128]{0:T(256)(128)(2,1)} %param.30) | copy-start | bytes 772
  7.3 454.5 %copy-start.10 = (bf16[2,1,128,1024]{3,2,1,0:T(8,128)(2,1)S(1)}, bf16[2,1,128,1024]{3,2,1,0:T(8,128)(2,1)}, u32[]{:S(2)}) copy-start(bf16[2,1,128,1024]{3,2,1,0:T(8,128)(2,1)} %param.20) | copy-start | bytes 1572868
  7.3 454.5 %copy-start.50 = (s32[2,1]{0,1:T(1,128)S(1)}, s32[2,1]{0,1:T(1,128)}, u32[]{:S(2)}) copy-start(s32[2,1]{0,1:T(1,128)} %param.22) | copy-start | bytes 28
  7.3 139.0 %all-gather.26.cloned.1.call-start = ((), (), s32[]{:S(2)}) async-start(), calls=%async_computation.8 | async-start | bytes 2359296 | tf_op jit(solution)/shard_map/all_gather | solution.py:119
  8.0 138.3 %all-gather.28.cloned.1.call-start = ((), (), s32[]{:S(2)}) async-start(), calls=%async_computation.9 | async-start | bytes 2359296 | tf_op jit(solution)/shard_map/all_gather | solution.py:118
  8.8 151.9 %all-gather.30.cloned.1.call-start = ((), (), s32[]{:S(2)}) async-start(), calls=%async_computation.10 | async-start | bytes 2359296 | tf_op jit(solution)/shard_map/all_gather | solution.py:120
  9.5 201.0 %all-gather.32.cloned.1.call-start = ((), (), s32[]{:S(2)}) async-start(), calls=%async_computation.11 | async-start | bytes 2359296 | tf_op jit(solution)/shard_map/all_gather | solution.py:121
  10.1 326.6 %all-gather.34.cloned.1.call-start = ((), (), s32[]{:S(2)}) async-start(), calls=%async_computation.12 | async-start | bytes 9437184 | tf_op jit(solution)/shard_map/all_gather | solution.py:129
  10.7 451.1 %all-gather.36.cloned.1.call-start = ((), (), s32[]{:S(2)}) async-start(), calls=%async_computation.13 | async-start | bytes 9437184 | tf_op jit(solution)/shard_map/all_gather | solution.py:131
  461.8 18.7 %all-gather.38.cloned.1.call-start = ((), (), s32[]{:S(2)}) async-start(), calls=%async_computation.21 | async-start | bytes 1310720 | tf_op jit(solution)/shard_map/while/body/eval_jaxpr/all_gather | solution.py:163
  464.6 34.8 %all-gather.40.cloned.1.call-start = ((), (), s32[]{:S(2)}) async-start(), calls=%async_computation.22 | async-start | bytes 1310720 | tf_op jit(solution)/shard_map/while/body/eval_jaxpr/all_gather | solution.py:166
  467.6 122.5 %reduce-scatter.29.cloned.1.call-start = ((), (), s32[]{:S(2)}) async-start(), calls=%async_computation.23 | async-start | bytes 1310720 | tf_op jit(solution)/shard_map/while
  470.2 48.2 %copy-start.31 = (f32[128]{0:T(128)}, f32[128]{0:T(128)S(1)}, u32[]{:S(2)}) copy-start(f32[128]{0:T(128)S(1)} %compare_convert_fusion.2) | copy-start | bytes 1540 | tf_op jit(solution)/shard_map/while
  547.8 52.1 %reduce-scatter.31.cloned.1.call-start = ((), (), s32[]{:S(2)}) async-start(), calls=%async_computation.24 | async-start | bytes 1310720 | tf_op jit(solution)/shard_map/while
  609.8 45.8 %copy-start.37 = (f32[4096]{0:T(1024)}, f32[4096]{0:T(1024)S(1)}, u32[]{:S(2)}) copy-start(f32[4096]{0:T(1024)S(1)} %get-tuple-element.900) | copy-start | bytes 49156 | tf_op jit(solution)/shard_map/while
  609.8 20.2 %all-gather.38.cloned.1.call-start = ((), (), s32[]{:S(2)}) async-start(), calls=%async_computation.21 | async-start | bytes 1310720 | tf_op jit(solution)/shard_map/while/body/eval_jaxpr/all_gather | solution.py:163
  612.6 36.1 %all-gather.40.cloned.1.call-start = ((), (), s32[]{:S(2)}) async-start(), calls=%async_computation.22 | async-start | bytes 1310720 | tf_op jit(solution)/shard_map/while/body/eval_jaxpr/all_gather | solution.py:166
  615.5 139.4 %reduce-scatter.29.cloned.1.call-start = ((), (), s32[]{:S(2)}) async-start(), calls=%async_computation.23 | async-start | bytes 1310720 | tf_op jit(solution)/shard_map/while
  618.1 49.5 %copy-start.31 = (f32[128]{0:T(128)}, f32[128]{0:T(128)S(1)}, u32[]{:S(2)}) copy-start(f32[128]{0:T(128)S(1)} %compare_convert_fusion.2) | copy-start | bytes 1540 | tf_op jit(solution)/shard_map/while
  697.1 59.6 %reduce-scatter.31.cloned.1.call-start = ((), (), s32[]{:S(2)}) async-start(), calls=%async_computation.24 | async-start | bytes 1310720 | tf_op jit(solution)/shard_map/while
  770.5 91.6 %reduce-scatter.17.cloned.1.call-start = ((), (), s32[]{:S(2)}) async-start(), calls=%async_computation.14 | async-start | bytes 4718592 | tf_op jit(solution)/shard_map/reduce_scatter | solution.py:64
  771.1 182.8 %reduce-scatter.19.cloned.1.call-start = ((), (), s32[]{:S(2)}) async-start(), calls=%async_computation.15 | async-start | bytes 4718592 | tf_op jit(solution)/shard_map/reduce_scatter | solution.py:65
  771.7 273.6 %reduce-scatter.21.cloned.1.call-start = ((), (), s32[]{:S(2)}) async-start(), calls=%async_computation.16 | async-start | bytes 4718592 | tf_op jit(solution)/shard_map/reduce_scatter | solution.py:66
  772.3 364.6 %reduce-scatter.23.cloned.1.call-start = ((), (), s32[]{:S(2)}) async-start(), calls=%async_computation.17 | async-start | bytes 4718592 | tf_op jit(solution)/shard_map/reduce_scatter | solution.py:67
  772.8 650.3 %reduce-scatter.25.cloned.1.call-start = ((), (), s32[]{:S(2)}) async-start(), calls=%async_computation.18 | async-start | bytes 18874368 | tf_op jit(solution)/shard_map/reduce_scatter | solution.py:45
  773.6 935.4 %reduce-scatter.27.cloned.1.call-start = ((), (), s32[]{:S(2)}) async-start(), calls=%async_computation.19 | async-start | bytes 18874368 | tf_op jit(solution)/shard_map/reduce_scatter | solution.py:47
  774.2 1007.0 %all-reduce.14.cloned.1.call-start = ((), (), s32[]{:S(2)}) async-start(), calls=%async_computation.20 | async-start | bytes 6291456 | tf_op jit(solution)/shard_map/psum | solution.py:75
  (86 other events, 438.0 us)
Sparse Core Ops, SparseCore 0:
  10.3 50.4 all-gather.25
  62.9 47.8 all-gather.27
  112.9 47.8 all-gather.29
  162.7 47.7 all-gather.31
  212.5 124.1 all-gather.33
  338.6 123.1 all-gather.35
  464.8 15.6 all-gather.37
  482.6 16.7 all-gather.39
  547.9 24.4 reduce-scatter.28
  575.0 24.8 reduce-scatter.30
  612.7 17.1 all-gather.37
  631.9 16.7 all-gather.39
  697.2 24.4 reduce-scatter.28
  725.3 24.4 reduce-scatter.30
  774.7 87.4 reduce-scatter.16
  866.0 87.8 reduce-scatter.18
  957.4 87.8 reduce-scatter.20
  1049.2 87.6 reduce-scatter.22
  1140.7 282.3 reduce-scatter.24
  1427.2 281.7 reduce-scatter.26
  1712.9 68.2 all-reduce.13
where the time goes:
time: 1820 us; the launch traced here: 1800 us
  waiting for transfers between devices  1330 us (73%)
  blocking collectives  176 us (10%)
  matrix products  171 us (9%)
  local copies, waits for them, and re-layouts  64 us (4%)
  other arithmetic  37.9 us (2%)
    reduce_scatter x1, waiting for transfers between devices, reduce_feedforward(): lax.psum_scatter(parts[0], 'fsdp', scatter_dimension=0, tiled=True)  284 us
    reduce_scatter x1, waiting for transfers between devices, reduce_feedforward(): lax.psum_scatter(parts[2], 'fsdp', scatter_dimension=0, tiled=True)  283 us
    all_gather x1, waiting for transfers between devices, body(): lax.all_gather(inner_weight, 'fsdp', axis=0, tiled=True)  126 us
    all_gather x1, waiting for transfers between devices, body(): lax.all_gather(outer_weight, 'fsdp', axis=0, tiled=True)  125 us
    reduce_scatter x1, waiting for transfers between devices, reduce_attention(): lax.psum_scatter(parts[1], 'fsdp', scatter_dimension=0, tiled=True)  90 us
    reduce_scatter x1, waiting for transfers between devices, reduce_attention(): lax.psum_scatter(parts[3], 'fsdp', scatter_dimension=0, tiled=True)  89.8 us
    reduce_scatter x1, waiting for transfers between devices, reduce_attention(): lax.psum_scatter(parts[2], 'fsdp', scatter_dimension=0, tiled=True)  89.6 us
    reduce_scatter x1, waiting for transfers between devices, reduce_attention(): lax.psum_scatter(parts[0], 'fsdp', scatter_dimension=0, tiled=True)  87.9 us
  transfers between devices with their start and end apart: 21, of which 16 were waited for; matrix products, arithmetic and copies ran while one was open for 8% of the time, Pallas kernels for 0%

commit v1 on v0

v1 whole, which is shorter than its diff:
```python
import jax
import jax.numpy as jnp
from jax import lax
from jax.sharding import PartitionSpec as P

HEAD_DIM = 64
EPSILON = 1e-06
F32 = jnp.float32
BF16 = jnp.bfloat16


def exact_gelu(hidden):
    return jax.nn.gelu(hidden, approximate=False)


def plain_product(left, right):
    return jnp.dot(left, right, preferred_element_type=F32)


def left_product(left, right):
    return lax.dot_general(left, right, (((0,), (0,)), ((), ())), preferred_element_type=F32)


def right_product(left, right):
    return lax.dot_general(left, right, (((1,), (1,)), ((), ())), preferred_element_type=F32)


def column_sums(rows):
    return jnp.sum(rows.astype(F32), axis=0)


def norm_parts(total):
    average = jnp.mean(total, axis=-1, keepdims=True)
    centered = total - average
    variance = jnp.mean(centered * centered, axis=-1, keepdims=True)
    rate = lax.rsqrt(variance + EPSILON)
    return centered * rate, rate


def norm_back(unit, rate, grad):
    return rate * (
        grad
        - jnp.mean(grad, axis=-1, keepdims=True)
        - unit * jnp.mean(grad * unit, axis=-1, keepdims=True)
    )


def split_columns(packed, widths):
    pieces = []
    start = 0
    for width in widths:
        pieces.append(packed[..., start : start + width])
        start += width
    return pieces


def attention_forward(queries, keys_all, values_all, key_valid, heads):
    shape = queries.shape[:2] + (heads, HEAD_DIM)
    key_shape = keys_all.shape[:2] + (heads, HEAD_DIM)
    scores = jnp.einsum(
        "sqhd,skhd->shqk",
        queries.reshape(shape),
        keys_all.reshape(key_shape),
        preferred_element_type=F32,
    ) * (HEAD_DIM**-0.5)
    scores = jnp.where(key_valid[:, None, None, :], scores, -1e30)
    top = jnp.max(scores, axis=-1, keepdims=True)
    weights = jnp.exp(scores - top)
    probs = (weights / jnp.sum(weights, axis=-1, keepdims=True)).astype(BF16)
    context = jnp.einsum(
        "shqk,skhd->sqhd", probs, values_all.reshape(key_shape), preferred_element_type=F32
    )
    return context.reshape(queries.shape).astype(BF16), probs


def attention_backward(queries, keys_all, values_all, probs, context_grad, heads):
    shape = queries.shape[:2] + (heads, HEAD_DIM)
    key_shape = keys_all.shape[:2] + (heads, HEAD_DIM)
    scale = HEAD_DIM**-0.5
    grad_heads = context_grad.reshape(shape)
    wide = probs.astype(F32)
    probs_grad = jnp.einsum(
        "sqhd,skhd->shqk", grad_heads, values_all.reshape(key_shape), preferred_element_type=F32
    )
    inner_total = jnp.sum(wide * probs_grad, axis=-1, keepdims=True)
    scores_grad = (wide * (probs_grad - inner_total)).astype(BF16)
    query_grad = jnp.einsum(
        "shqk,skhd->sqhd", scores_grad, keys_all.reshape(key_shape), preferred_element_type=F32
    )
    key_part = jnp.einsum(
        "shqk,sqhd->skhd", scores_grad, queries.reshape(shape), preferred_element_type=F32
    )
    value_part = jnp.einsum("shqk,sqhd->skhd", probs, grad_heads, preferred_element_type=F32)
    return (
        (query_grad * scale).astype(BF16).reshape(queries.shape),
        (key_part * scale).astype(BF16).reshape(keys_all.shape),
        value_part.astype(BF16).reshape(values_all.shape),
    )


def gather_rows(part):
    return lax.all_gather(part, "fsdp", axis=0, tiled=True)


def reduce_rows(part):
    share = lax.psum_scatter(part.astype(BF16), "fsdp", scatter_dimension=0, tiled=True)
    return lax.psum(share, "ctx").astype(F32)


def body(
    inputs,
    cotangent,
    lengths,
    query_weight,
    key_weight,
    value_weight,
    output_weight,
    query_bias,
    value_bias,
    output_bias,
    first_gain,
    first_shift,
    inner_weight,
    inner_bias,
    outer_weight,
    outer_bias,
    second_gain,
    second_shift,
):
    vectors = (
        query_bias,
        value_bias,
        output_bias,
        first_gain,
        first_shift,
        inner_bias,
        outer_bias,
        second_gain,
        second_shift,
    )
    widths = [member.shape[0] for member in vectors]
    packed = lax.all_gather(jnp.concatenate(vectors), "fsdp", axis=0, tiled=False)
    (
        bias_query,
        bias_value,
        bias_output,
        gain_first,
        shift_first,
        bias_inner,
        bias_outer,
        gain_second,
        shift_second,
    ) = [piece.reshape(-1).astype(F32) for piece in split_columns(packed, widths)]
    full_qkv = gather_rows(jnp.concatenate((query_weight, key_weight, value_weight), axis=1))
    full_output = gather_rows(output_weight)
    full_inner = gather_rows(inner_weight)
    full_outer = gather_rows(outer_weight)

    micro, seqs, block_len, width = inputs.shape
    heads = width // HEAD_DIM
    ctx_size = lax.axis_size("ctx")
    total_slots = block_len * ctx_size
    group = micro * seqs
    rows = group * block_len
    flat_len = lengths.reshape(group)
    local_pos = lax.axis_index("ctx") * block_len + jnp.arange(block_len, dtype=jnp.int32)
    row_mask = (local_pos[None, :] < flat_len[:, None]).astype(F32).reshape(rows, 1)
    key_valid = jnp.arange(total_slots, dtype=jnp.int32)[None, :] < flat_len[:, None]

    flat_rows = inputs.reshape(rows, width)
    qkv = plain_product(flat_rows, full_qkv)
    queries = (qkv[:, :width] + bias_query).astype(BF16)
    keys_values = jnp.concatenate(
        (qkv[:, width : 2 * width], qkv[:, 2 * width :] + bias_value), axis=1
    ).astype(BF16)
    keys_values_all = lax.all_gather(
        keys_values.reshape(group, block_len, 2 * width), "ctx", axis=1, tiled=True
    )
    keys_all = keys_values_all[:, :, :width]
    values_all = keys_values_all[:, :, width:]
    queries3 = queries.reshape(group, block_len, width)
    context, probs = attention_forward(queries3, keys_all, values_all, key_valid, heads)
    context = context.reshape(rows, width)

    first_sum = flat_rows.astype(F32) + plain_product(context, full_output) + bias_output
    first_unit, first_rate = norm_parts(first_sum)
    normed = first_unit * gain_first + shift_first
    normed_low = normed.astype(BF16)
    hidden = plain_product(normed_low, full_inner) + bias_inner
    active, gelu_back = jax.vjp(exact_gelu, hidden)
    active_low = active.astype(BF16)
    second_sum = normed + plain_product(active_low, full_outer) + bias_outer
    second_unit, second_rate = norm_parts(second_sum)
    output = ((second_unit * gain_second + shift_second) * row_mask).astype(BF16)

    out_grad = cotangent.reshape(rows, width).astype(F32) * row_mask
    second_gain_part = jnp.sum(out_grad * second_unit, axis=0)
    second_shift_part = jnp.sum(out_grad, axis=0)
    second_grad = norm_back(second_unit, second_rate, out_grad * gain_second)
    second_low = second_grad.astype(BF16)
    outer_weight_part = left_product(active_low, second_low).astype(BF16)
    outer_bias_part = column_sums(second_low)
    (hidden_grad,) = gelu_back(right_product(second_low, full_outer))
    hidden_low = hidden_grad.astype(BF16)
    inner_weight_part = left_product(normed_low, hidden_low).astype(BF16)
    inner_bias_part = column_sums(hidden_low)
    normed_grad = second_grad + right_product(hidden_low, full_inner)
    first_gain_part = jnp.sum(normed_grad * first_unit, axis=0)
    first_shift_part = jnp.sum(normed_grad, axis=0)
    first_grad = norm_back(first_unit, first_rate, normed_grad * gain_first)
    branch_low = first_grad.astype(BF16)
    output_weight_part = left_product(context, branch_low).astype(BF16)
    output_bias_part = column_sums(branch_low)
    context_grad = right_product(branch_low, full_output).astype(BF16)
    query_grad, key_part, value_part = attention_backward(
        queries3, keys_all, values_all, probs, context_grad.reshape(queries3.shape), heads
    )
    keys_values_grad = lax.psum_scatter(
        jnp.concatenate((key_part, value_part), axis=2), "ctx", scatter_dimension=1, tiled=True
    ).reshape(rows, 2 * width)
    qkv_grad = jnp.concatenate((query_grad.reshape(rows, width), keys_values_grad), axis=1)
    qkv_weight_part = left_product(flat_rows, qkv_grad).astype(BF16)
    query_bias_part = column_sums(qkv_grad[:, :width])
    value_bias_part = column_sums(qkv_grad[:, 2 * width :])
    input_grad = first_grad + right_product(qkv_grad, full_qkv)

    qkv_share = reduce_rows(qkv_weight_part)
    output_share = reduce_rows(output_weight_part)
    inner_share = reduce_rows(inner_weight_part)
    outer_share = reduce_rows(outer_weight_part)
    vector_parts = (
        query_bias_part,
        value_bias_part,
        output_bias_part,
        first_gain_part,
        first_shift_part,
        inner_bias_part,
        outer_bias_part,
        second_gain_part,
        second_shift_part,
    )
    fsdp_size = lax.axis_size("fsdp")
    packed_parts = jnp.concatenate(
        [part.reshape(fsdp_size, -1) for part in vector_parts], axis=1
    )
    vector_share = lax.psum(
        lax.psum_scatter(packed_parts, "fsdp", scatter_dimension=0, tiled=True), "ctx"
    )[0]
    shares = split_columns(vector_share, widths)
    query_share, key_share, value_share = split_columns(qkv_share, [width] * 3)
    return (
        output.reshape(inputs.shape),
        input_grad.reshape(inputs.shape),
        query_share,
        key_share,
        value_share,
        output_share,
        shares[0],
        shares[1],
        shares[2],
        shares[3],
        shares[4],
        inner_share,
        shares[5],
        outer_share,
        shares[6],
        shares[7],
        shares[8],
    )


def solution(mesh):
    data = P(None, "fsdp", "ctx", None)
    matrix = P("fsdp", None)
    vector = P("fsdp")
    return jax.shard_map(
        body,
        mesh=mesh,
        in_specs=(data, data, P(None, "fsdp"))
        + (matrix,) * 4
        + (vector,) * 5
        + (matrix, vector, matrix, vector, vector, vector),
        out_specs=(data, data)
        + (matrix,) * 4
        + (vector,) * 5
        + (matrix, vector, matrix, vector, vector, vector),
        check_vma=False,
    )
```

time: 1820 us -> 1160 us (0.64)
  waiting for transfers between devices: 1330 us -> 882 us
  blocking collectives: 176 us -> 67.2 us
  matrix products: 171 us -> 98.6 us
    reduce_scatter x6 -> x4, waiting for transfers between devices: 925 us -> 408 us  [the longest x3 374 us: reduce_rows(): lax.psum_scatter(part.astype(BF16), 'fsdp', scatter_dimension=0, tiled=True)]
    all_gather x9 -> x1, blocking collectives: 135 us -> 25.8 us  [body(): lax.all_gather(jnp.concatenate(vectors), 'fsdp', axis=0, tiled=False)]
    unnamed x13 -> x12, waiting for transfers between devices: 6.99 us -> 98.3 us
    while x176 -> x0, local copies, waits for them, and re-layouts: 50.6 us -> none
    dot_general x12 -> x4, matrix products: 71.9 us -> 22.4 us  [left_product(): lax.dot_general(left, right, (((0,), (0,)), ((), ())), preferred_element_...]
    unnamed x45 -> x70, local copies, waits for them, and re-layouts: 1.96 us -> 31.4 us
    dot_general x24 -> x9, matrix products: 68.8 us -> 42.9 us  [the longest x4 30.1 us: plain_product(): return jnp.dot(left, right, preferred_element_type=F32)]
    all_gather x10 -> x5, waiting for transfers between devices: 366 us -> 354 us  [the longest x4 325 us: gather_rows(): return lax.all_gather(part, 'fsdp', axis=0, tiled=True)]
  transfers between devices with their start and end apart: 21 -> 11, of which waited for: 16 -> 11; matrix products, arithmetic and copies ran while one was open for 8% -> 8% of each run, Pallas kernels for 0% -> 0%
where the time goes in v1:
time: 1160 us; the launch traced here: 1150 us
  waiting for transfers between devices  882 us (76%)
  matrix products  98.6 us (8%)
  blocking collectives  67.2 us (6%)
  local copies, waits for them, and re-layouts  63 us (5%)
  other arithmetic  24.7 us (2%)
  between operations  14.6 us (1%)
    reduce_scatter x3, waiting for transfers between devices, reduce_rows(): lax.psum_scatter(part.astype(BF16), 'fsdp', scatter_dimension=0, tiled=True)  374 us
    all_gather x4, waiting for transfers between devices, gather_rows(): return lax.all_gather(part, 'fsdp', axis=0, tiled=True)  325 us
    unnamed x12, waiting for transfers between devices  98.3 us
    reduce_scatter x1, waiting for transfers between devices, body(): lax.psum_scatter(jnp.concatenate((key_part, value_part), axis=2), 'ctx',...  34.5 us
    unnamed x70, local copies, waits for them, and re-layouts  31.4 us
    dot_general x4, matrix products, plain_product(): return jnp.dot(left, right, preferred_element_type=F32)  30.1 us
    all_gather x1, waiting for transfers between devices, body(): lax.all_gather(keys_values.reshape(group, block_len, 2 * width), 'ctx', a...  29 us
    unnamed x1, blocking collectives  28.6 us
  transfers between devices with their start and end apart: 11, of which 11 were waited for; matrix products, arithmetic and copies ran while one was open for 8% of the time, Pallas kernels for 0%

profile of v1, /device:TPU:1, one launch (start us, length us, event | category | flops | bytes accessed | tf_op | source)
XLA Modules:
  0.0 1151.0 jit_solution(14489153221293311323)
XLA Ops:
  16.9 25.8 %all-gather.1 = bf16[8,1,1536]{2,1,0:T(2,128)(2,1)S(1)} all-gather(bf16[1,1,1536]{2,1,0:T(2,128)(2,1)S(1)} %reshape.321), channel_id=2, replica_groups=mesh['ctx'=4,'fsdp'=8] {'fsdp'}, dimensions={0}, use_global_device_ids=true | all-gather | bytes 27648 | tf_op jit(solution)/shard_map/all_gather | solution.py:142
  42.8 69.2 %all-gather.8.cloned.1.call-done = bf16[1024,3072]{1,0:T(8,128)(2,1)} async-done(((bf16[128,3072]{1,0:T(8,128)(2,1)}), bf16[1024,3072]{1,0:T(8,128)(2,1)}) %all-gather.8.cloned.1.call-update) | async-done | bytes 6291472 | tf_op jit(solution)/shard_map/all_gather | solution.py:102
  112.0 4.8 convolution_bitcast_fusion
  123.0 29.0 %all-gather.10.cloned.1.call-done = bf16[2,512,2048]{2,1,0:T(8,128)(2,1)} async-done(((bf16[2,128,2048]{2,1,0:T(8,128)(2,1)}), bf16[2,512,2048]{2,1,0:T(8,128)(2,1)}) %all-gather.10.cloned.1.call-update) | async-done | bytes 4194320 | tf_op jit(solution)/shard_map/all_gather | solution.py:176
  151.9 4.2 fusion.52
  162.1 7.7 fusion.54
  169.8 3.9 divide_convert_fusion
  178.6 23.3 %all-gather.12.cloned.1.call-done = bf16[1024,1024]{1,0:T(8,128)(2,1)} async-done(((bf16[128,1024]{1,0:T(8,128)(2,1)}), bf16[1024,1024]{1,0:T(8,128)(2,1)}) %all-gather.12.cloned.1.call-update) | async-done | bytes 2097168 | tf_op jit(solution)/shard_map/all_gather | solution.py:102
  204.8 123.2 %all-gather.14.cloned.1.call-done = bf16[1024,4096]{1,0:T(8,128)(2,1)} async-done(((bf16[128,4096]{1,0:T(8,128)(2,1)}), bf16[1024,4096]{1,0:T(8,128)(2,1)}) %all-gather.14.cloned.1.call-update) | async-done | bytes 8388624 | tf_op jit(solution)/shard_map/all_gather | solution.py:102
  328.0 16.2 %multiply_convert_fusion.1 = (bf16[256,4096]{1,0:T(8,128)(2,1)}, f32[256,4096]{1,0:T(8,128)}, f32[256,4096]{1,0:T(8,128)}) fusion(f32[4096]{0:T(1024)S(1)} %bitcast.181, bf16[1024,4096]{1,0:T(8,128)(2,1)} %all-gather.14.cloned.1.call-done, f32[256,1024]{1,0:T(8,128)S(1)} %get-tuple-element.115, f32[1024]{0:T(1024)S(1)} %get-tuple-element.97, ...), kind=kOutput, calls=%fused_computation.19 | convolution fusion | flops 2218000384 | bytes 19949568 | tf_op jit(solution)/shard_map/dot_general | solution.py:17
  344.2 108.9 %all-gather.16.cloned.1.call-done = bf16[4096,1024]{1,0:T(8,128)(2,1)} async-done(((bf16[512,1024]{1,0:T(8,128)(2,1)}), bf16[4096,1024]{1,0:T(8,128)(2,1)}) %all-gather.16.cloned.1.call-update) | async-done | bytes 8388624 | tf_op jit(solution)/shard_map/all_gather | solution.py:102
  453.1 6.5 fusion.56
  461.9 11.1 convert_reduce_fusion
  473.0 6.9 multiply_reduce_fusion.1
  488.3 4.0 fusion.1
  493.0 4.3 fusion.2
  501.3 3.9 copy.74
  507.6 4.7 pad_maximum_fusion
  513.9 4.5 convert_reduce_fusion.4
  521.1 34.5 %reduce-scatter.8.cloned.1.call-done = bf16[2,128,2048]{2,1,0:T(8,128)(2,1)} async-done(((bf16[2,512,2048]{2,1,0:T(8,128)(2,1)}), bf16[2,128,2048]{2,1,0:T(8,128)(2,1)}) %reduce-scatter.8.cloned.1.call-update) | async-done | bytes 1048592 | tf_op jit(solution)/shard_map/reduce_scatter | solution.py:218
  555.6 5.9 convert_bitcast_fusion
  561.5 8.7 copy.83
  573.9 7.3 convolution_convert_fusion.1
  582.4 7.2 convolution_convert_fusion
  591.1 96.5 %reduce-scatter.16.cloned.1.call-done = bf16[128,3072]{1,0:T(8,128)(2,1)} async-done(((bf16[1024,3072]{1,0:T(8,128)(2,1)}), bf16[128,3072]{1,0:T(8,128)(2,1)}) %reduce-scatter.16.cloned.1.call-update) | async-done | bytes 786448
  689.8 68.2 %reduce-scatter.10.cloned.1.call-done = bf16[128,1024]{1,0:T(8,128)(2,1)} async-done(((bf16[1024,1024]{1,0:T(8,128)(2,1)}), bf16[128,1024]{1,0:T(8,128)(2,1)}) %reduce-scatter.10.cloned.1.call-update) | async-done | bytes 262160 | tf_op jit(solution)/shard_map/reduce_scatter | solution.py:106
  758.0 154.0 %reduce-scatter.12.cloned.1.call-done = bf16[128,4096]{1,0:T(8,128)(2,1)} async-done(((bf16[1024,4096]{1,0:T(8,128)(2,1)}), bf16[128,4096]{1,0:T(8,128)(2,1)}) %reduce-scatter.12.cloned.1.call-update) | async-done | bytes 1048592 | tf_op jit(solution)/shard_map/reduce_scatter | solution.py:106
  912.1 151.5 %reduce-scatter.14.cloned.1.call-done = bf16[512,1024]{1,0:T(8,128)(2,1)} async-done(((bf16[4096,1024]{1,0:T(8,128)(2,1)}), bf16[512,1024]{1,0:T(8,128)(2,1)}) %reduce-scatter.14.cloned.1.call-update) | async-done | bytes 1048592 | tf_op jit(solution)/shard_map/reduce_scatter | solution.py:106
  1063.6 28.6 %all-reduce = f32[8,1536]{1,0:T(8,128)S(1)} all-reduce(f32[8,1536]{1,0:T(8,128)S(1)} %constant_dynamic-update-slice_fusion), channel_id=6, replica_groups=mesh['ctx'=4,'fsdp'=8] {'fsdp'}, use_global_device_ids=true, to_apply=%region_25.26.clone | all-reduce | flops 12288 | bytes 98304
  1092.9 12.7 %psum.37 = f32[1,1536]{1,0:T(1,128)S(1)} all-reduce(f32[1,1536]{1,0:T(1,128)S(1)} %constant_dynamic-slice_fusion), channel_id=1, replica_groups=mesh['ctx'=4,'fsdp'=8] {'ctx'}, use_global_device_ids=true, to_apply=%region_26.27 | all-reduce | flops 1536 | bytes 12288 | tf_op jit(solution)/shard_map/psum | solution.py:246
  1106.8 6.0 convolution_add_fusion.2
  1112.8 22.0 %all-reduce.4.cloned.1.call-done = (bf16[128,3072]{0,1:T(8,128)(2,1)}, bf16[128,1024]{1,0:T(8,128)(2,1)}, bf16[128,4096]{1,0:T(8,128)(2,1)}, bf16[512,1024]{1,0:T(8,128)(2,1)}) async-done(((bf16[128,3072]{0,1:T(8,128)(2,1)}, bf16[128,1024]{1,0:T(8,128)(2,1)}, bf16[128,4096]{1,0:T(8,128)(2,1)}, bf16[512,1024]{1,0:T(8,128)(2,1)}), (bf16[128,3072]{0,1:T(8,128)(2,1)}, bf16[128,1024]{1,0:T(8,128)(2,1)}, ...) | async-done | bytes 3145744 | tf_op jit(solution)/shard_map/psum | solution.py:107
  (141 shorter events, 71.1 us)
Async XLA Ops:
  7.2 104.8 %all-gather.8.cloned.1.call-start = ((), (), s32[]{:S(2)}) async-start(), calls=%async_computation.5 | async-start | bytes 7077888 | tf_op jit(solution)/shard_map/all_gather | solution.py:102
  9.3 142.6 %all-gather.10.cloned.1.call-start = ((), (), s32[]{:S(2)}) async-start(), calls=%async_computation.6 | async-start | bytes 5242880 | tf_op jit(solution)/shard_map/all_gather | solution.py:176
  116.8 3.4 copy-start.19
  116.9 3.4 copy-start.8
  118.2 83.7 %all-gather.12.cloned.1.call-start = ((), (), s32[]{:S(2)}) async-start(), calls=%async_computation.7 | async-start | bytes 2359296 | tf_op jit(solution)/shard_map/all_gather | solution.py:102
  118.9 209.1 %all-gather.14.cloned.1.call-start = ((), (), s32[]{:S(2)}) async-start(), calls=%async_computation.8 | async-start | bytes 9437184 | tf_op jit(solution)/shard_map/all_gather | solution.py:102
  119.5 333.6 %all-gather.16.cloned.1.call-start = ((), (), s32[]{:S(2)}) async-start(), calls=%async_computation.9 | async-start | bytes 9437184 | tf_op jit(solution)/shard_map/all_gather | solution.py:102
  120.1 435.5 %reduce-scatter.8.cloned.1.call-start = ((), (), s32[]{:S(2)}) async-start(), calls=%async_computation.10 | async-start | bytes 5242880 | tf_op jit(solution)/shard_map/reduce_scatter | solution.py:218
  159.1 2.9 copy-start.14
  173.7 2.0 copy-start
  453.1 6.8 copy-start.9
  459.7 2.2 copy-start.21
  461.8 11.2 copy-start.11
  473.0 6.9 copy-start.13
  473.0 8.3 copy-start.5
  480.3 1.0 copy-start.3
  488.3 4.0 copy-start.1
  488.3 4.0 copy-start.10
  493.0 6.2 copy-start.15
  497.3 1.9 copy-start.2
  512.3 1.6 copy-start.6
  512.4 175.2 %reduce-scatter.16.cloned.1.call-start = ((), (), s32[]{:S(2)}) async-start(), calls=%async_computation.14 | async-start | bytes 7077888
  570.1 1.2 copy-start.4
  570.1 1.4 copy-start.7
  570.2 187.9 %reduce-scatter.10.cloned.1.call-start = ((), (), s32[]{:S(2)}) async-start(), calls=%async_computation.11 | async-start | bytes 2359296 | tf_op jit(solution)/shard_map/reduce_scatter | solution.py:106
  573.6 338.5 %reduce-scatter.12.cloned.1.call-start = ((), (), s32[]{:S(2)}) async-start(), calls=%async_computation.12 | async-start | bytes 9437184 | tf_op jit(solution)/shard_map/reduce_scatter | solution.py:106
  581.2 1.2 copy-start.12
  581.2 482.4 %reduce-scatter.14.cloned.1.call-start = ((), (), s32[]{:S(2)}) async-start(), calls=%async_computation.13 | async-start | bytes 9437184 | tf_op jit(solution)/shard_map/reduce_scatter | solution.py:106
  589.6 1.3 copy-start.18
  589.7 545.1 %all-reduce.4.cloned.1.call-start = ((), (), s32[]{:S(2)}) async-start(), calls=%async_computation.15 | async-start | bytes 6291456 | tf_op jit(solution)/shard_map/psum | solution.py:107
  1134.8 7.1 copy-start.16
  1137.1 6.3 copy-start.17
  (1 other events, 0.7 us)
Sparse Core Ops, SparseCore 0:
  10.8 101.1 all-gather.7
  118.3 33.5 all-gather.9
  154.1 47.7 all-gather.11
  203.9 124.1 all-gather.13
  330.0 123.1 all-gather.15
  512.5 43.0 reduce-scatter.7
  570.3 117.2 reduce-scatter.15
  692.1 65.9 reduce-scatter.9
  762.1 149.9 reduce-scatter.11
  915.5 147.9 reduce-scatter.13
  1066.9 67.8 all-reduce.3

commit v2 on v1

--- a/solution.py
+++ b/solution.py
@@ -1,12 +1,812 @@
+import functools
+
 import jax
 import jax.numpy as jnp
 from jax import lax
+from jax.experimental import pallas as pl
+from jax.experimental.pallas import tpu as pltpu
 from jax.sharding import PartitionSpec as P
 
 HEAD_DIM = 64
 EPSILON = 1e-06
 F32 = jnp.float32
 BF16 = jnp.bfloat16
+MESH = pl.DeviceIdType.MESH
+LINE = 4
+PAIR = 2
+
+
+class Place:
+    def __init__(self):
+        self.ctx = lax.axis_index("ctx")
+        self.shard = lax.axis_index("fsdp")
+        self.side = lax.div(self.ctx, 2)
+        self.core = lax.rem(self.ctx, 2)
+        self.line = lax.div(self.shard, PAIR)
+        self.pair = lax.rem(self.shard, PAIR)
+
+    def ahead(self, way):
+        return (self.ctx, self.shard + way * PAIR)
+
+    def across(self):
+        return (self.ctx, self.shard + 1 - 2 * self.pair)
+
+    def beside(self):
+        return (self.ctx + 2 - 4 * self.side, self.shard)
+
+    def twin(self):
+        return (self.ctx + 1 - 2 * self.core, self.shard)
+
+    def has(self, way, steps):
+        if steps == 0:
+            return None
+        return self.line >= steps if way > 0 else self.line <= LINE - 1 - steps
+
+    def can(self, way):
+        return self.line <= LINE - 2 if way > 0 else self.line >= 1
+
+    def shard_of(self, way, steps, other):
+        pair = 1 - self.pair if other else self.pair
+        return (self.line - way * steps) * PAIR + pair
+
+
+def when(conditions, action):
+    held = [c for c in conditions if c is not None]
+    if not held:
+        action()
+        return
+    both = held[0]
+    for c in held[1:]:
+        both = jnp.logical_and(both, c)
+    pl.when(both)(action)
+
+
+def greet(place):
+    barrier = pltpu.get_barrier_semaphore()
+    for peer in (place.across(), place.beside(), place.twin()):
+        pl.semaphore_signal(barrier, inc=1, device_id=peer, device_id_type=MESH)
+    for way in (1, -1):
+        when(
+            [place.can(way)],
+            lambda way=way: pl.semaphore_signal(
+                barrier, inc=1, device_id=place.ahead(way), device_id_type=MESH
+            ),
+        )
+    lines = jnp.minimum(place.line, 1) + jnp.minimum(LINE - 1 - place.line, 1)
+    pl.semaphore_wait(barrier, 3 + lines)
+
+
+class Flow:
+    def __init__(self, array, shard_rows, region, order="line", sides=False, cores=True):
+        self.array = array
+        self.shard_rows = shard_rows
+        self.region = region
+        self.order = order
+        self.sides = sides
+        self.cores = cores
+
+    def view(self, ref, shard, core, side):
+        row, rows, column, columns = self.region(core, side)
+        start = row if shard is None else shard * self.shard_rows + row
+        if not isinstance(start, int):
+            start = pl.multiple_of(start, 16)
+        if not isinstance(column, int):
+            column = pl.multiple_of(column, 128)
+        return ref.at[pl.ds(start, rows), pl.ds(column, columns)]
+
+
+def positions(order):
+    found = []
+    if order == "line":
+        found.append(("P", 1, 0, True))
+        for steps in range(1, LINE):
+            for way in (1, -1):
+                found.append(("L", way, steps, False))
+                found.append(("P", way, steps, True))
+    else:
+        found.append(("P", 1, 0, True))
+        for steps in range(1, LINE):
+            for way in (1, -1):
+                found.append(("L", way, steps, False))
+                found.append(("L", way, steps, True))
+    return found
+
+
+class Labels:
+    def __init__(self):
+        self.numbers = {}
+
+    def __call__(self, key):
+        return self.numbers.setdefault(key, len(self.numbers))
+
+
+def gather_labels(flows):
+    labels = Labels()
+    for number, flow in enumerate(flows):
+        for spot in positions(flow.order):
+            labels((number, "in") + spot)
+            if flow.sides:
+                labels((number, "side") + spot)
+            if flow.cores:
+                labels((number, "twin") + spot)
+                if flow.sides:
+                    labels((number, "twinside") + spot)
+    return labels
+
+
+class Gather:
+    def __init__(self, place, flows, owns, fulls, send, recv):
+        self.place, self.flows, self.owns, self.fulls = place, flows, owns, fulls
+        self.send, self.recv = send, recv
+        self.labels = gather_labels(flows)
+        self.sent = []
+
+    def copy(self, number, key, spot, peer, core, side, own=False):
+        flow = self.flows[number]
+        place = self.place
+        if own:
+            shard = place.shard
+            source = flow.view(self.owns[flow.array], None, core, side)
+        else:
+            shard = place.shard_of(*spot[1:])
+            source = flow.view(self.fulls[flow.array], shard, core, side)
+        target = flow.view(self.fulls[flow.array], shard, core, side)
+        label = self.labels((number,) + key)
+        return pltpu.make_async_remote_copy(
+            source,
+            target,
+            self.send.at[label],
+            self.recv.at[label],
+            device_id=peer,
+            device_id_type=MESH,
+        )
+
+    def start(self, conditions, copy):
+        when(conditions, copy.start)
+        self.sent.append((conditions, copy))
+
+    def begin(self, number):
+        flow, place = self.flows[number], self.place
+        core, side = place.core, place.side
+        here = (None, 1, 0, False)
+        for way in (1, -1):
+            self.start(
+                [place.can(way)],
+                self.copy(
+                    number, ("in", "L", way, 1, False), here, place.ahead(way), core, side, True
+                ),
+            )
+        self.start(
+            [],
+            self.copy(number, ("in", "P", 1, 0, True), here, place.across(), core, side, True),
+        )
+
+    def arrive(self, number, spot):
+        flow, place = self.flows[number], self.place
+        kind, way, steps, other = spot
+        core, side = place.core, place.side
+        there = place.has(way, steps)
+
+        def take():
+            self.copy(number, ("in",) + spot, spot, place.across(), core, side).wait_recv()
+
+        when([there], take)
+
+        def onward(extra, key, peer):
+            self.start(
+                [c for c in (there, extra) if c is not None],
+                self.copy(number, key, spot, peer, core, side),
+            )
+
+        if kind == "L" and steps + 1 < LINE:
+            onward(place.can(way), ("in", "L", way, steps + 1, other), place.ahead(way))
+        if kind == "L" and flow.order == "line":
+            onward(None, ("in", "P", way, steps, True), place.across())
+        if kind == "P" and flow.order == "pair":
+            for direction in (1, -1):
+                onward(
+                    place.can(direction), ("in", "L", direction, 1, True), place.ahead(direction)
+                )
+        if flow.sides:
+            onward(None, ("side",) + spot, place.beside())
+        if flow.cores:
+            onward(None, ("twin",) + spot, place.twin())
+
+    def arrive_side(self, number, spot):
+        flow, place = self.flows[number], self.place
+        there = place.has(*spot[1:3])
+        core, side = place.core, 1 - place.side
+        when(
+            [there],
+            lambda: self.copy(
+                number, ("side",) + spot, spot, place.beside(), core, side
+            ).wait_recv(),
+        )
+        if flow.cores:
+            self.start(
+                [there] if there is not None else [],
+                self.copy(number, ("twinside",) + spot, spot, place.twin(), core, side),
+            )
+
+    def arrive_twin(self, number, spot):
+        flow, place = self.flows[number], self.place
+        there = place.has(*spot[1:3])
+        core = 1 - place.core
+        if flow.cores:
+            when(
+                [there],
+                lambda: self.copy(
+                    number, ("twin",) + spot, spot, place.twin(), core, place.side
+                ).wait_recv(),
+            )
+            if flow.sides:
+                when(
+                    [there],
+                    lambda: self.copy(
+                        number, ("twinside",) + spot, spot, place.twin(), core, 1 - place.side
+                    ).wait_recv(),
+                )
+
+    def steps(self, flow_order=None):
+        order = list(range(len(self.flows)))
+        todo = [lambda n=n: self.begin(n) for n in order]
+        late = []
+        spots = {n: positions(self.flows[n].order) for n in order}
+        for index in range(len(positions("line"))):
+            for n in order:
+                spot = spots[n][index]
+                todo.append(lambda n=n, spot=spot: self.arrive(n, spot))
+                if self.flows[n].sides:
+                    late.append((index, n, spot))
+            ready = [entry for entry in late if entry[0] < index - 1]
+            late = [entry for entry in late if entry[0] >= index - 1]
+            for _, n, spot in ready:
+                todo.append(lambda n=n, spot=spot: self.arrive_side(n, spot))
+        for _, n, spot in late:
+            todo.append(lambda n=n, spot=spot: self.arrive_side(n, spot))
+        return todo
+
+    def finish(self):
+        for number, flow in enumerate(self.flows):
+            for spot in positions(flow.order):
+                self.arrive_twin(number, spot)
+        for conditions, copy in self.sent:
+            when(conditions, copy.wait_send)
+
+
+def gather_kernel(flows, count, *refs):
+    owns, fulls = refs[:count], refs[count : 2 * count]
+    send, recv, local = refs[2 * count :]
+    place = Place()
+    keep = [
+        pltpu.make_async_copy(
+            owns[k], fulls[k].at[pl.ds(place.shard * owns[k].shape[0], owns[k].shape[0]), :], local.at[k]
+        )
+        for k in range(count)
+    ]
+    greet(place)
+    work = Gather(place, flows, owns, fulls, send, recv)
+    for copy in keep:
+        copy.start()
+    for step in work.steps():
+        step()
+    work.finish()
+    for copy in keep:
+        copy.wait()
+
+
+def gather_call(arrays, flows, shards, collective_id):
+    labels = gather_labels(flows)
+    count = len(arrays)
+    return pl.pallas_call(
+        functools.partial(gather_kernel, flows, count),
+        out_shape=[
+            jax.ShapeDtypeStruct((shards * a.shape[0], a.shape[1]), a.dtype) for a in arrays
+        ],
+        in_specs=[pl.BlockSpec(memory_space=pltpu.VMEM)] * count,
+        out_specs=[pl.BlockSpec(memory_space=pl.ANY)] * count,
+        scratch_shapes=[
+            pltpu.SemaphoreType.DMA((len(labels.numbers),)),
+            pltpu.SemaphoreType.DMA((len(labels.numbers),)),
+            pltpu.SemaphoreType.DMA((count,)),
+        ],
+        compiler_params=pltpu.CompilerParams(collective_id=collective_id, has_side_effects=True),
+        name="gather_weights",
+    )(*arrays)
+
+
+def column_flows(array, shard_rows, columns, shared, early):
+    half = columns // 2
+    part = (half - shared) // 2
+    flows = []
+    if shared:
+        flows.append(
+            Flow(array, shard_rows, lambda core, side: (0, shard_rows, core * half, shared))
+        )
+    if early:
+        flows.append(
+            Flow(
+                array,
+                shard_rows,
+                lambda core, side: (0, shard_rows, core * half + shared + side * part, early),
+                sides=True,
+            )
+        )
+    if part > early:
+        flows.append(
+            Flow(
+                array,
+                shard_rows,
+                lambda core, side: (
+                    0,
+                    shard_rows,
+                    core * half + shared + side * part + early,
+                    part - early,
+                ),
+                order="pair",
+                sides=True,
+            )
+        )
+    return flows
+
+
+def row_flows(array, shard_rows, columns, shared, early):
+    half = shard_rows // 2
+    part = (half - shared) // 2
+    return [
+        Flow(array, shard_rows, lambda core, side: (core * half, shared, 0, columns)),
+        Flow(
+            array,
+            shard_rows,
+            lambda core, side: (core * half + shared + side * part, early, 0, columns),
+            sides=True,
+        ),
+        Flow(
+            array,
+            shard_rows,
+            lambda core, side: (core * half + shared + side * part + early, part - early, 0, columns),
+            order="pair",
+            sides=True,
+        ),
+    ]
+
+
+class Part:
+    def __init__(self, rows, columns, along, flows, dtype=BF16):
+        self.rows, self.columns, self.along, self.dtype = rows, columns, along, dtype
+        self.flows = flows
+        self.half_rows = rows // 2 if along == "rows" else rows
+        self.half_columns = columns // 2 if along == "columns" else columns
+
+    def half(self, ref, shard, core):
+        base = 0 if shard is None else pl.multiple_of(shard * self.rows, 16)
+        if self.along == "rows":
+            row = core * self.half_rows + (0 if shard is None else shard * self.rows)
+            return ref.at[pl.ds(pl.multiple_of(row, 16), self.half_rows), :]
+        if self.along == "columns":
+            column = pl.multiple_of(core * self.half_columns, 128)
+            return ref.at[pl.ds(base, self.rows), pl.ds(column, self.half_columns)]
+        return ref.at[pl.ds(base, self.rows), :]
+
+    def inner(self, flow, side):
+        first, extent = flow[0](side), flow[1]
+        if self.along == "rows":
+            start = first if isinstance(first, int) else pl.multiple_of(first, 16)
+            return pl.ds(start, extent), slice(None)
+        start = first if isinstance(first, int) else pl.multiple_of(first, 128)
+        return slice(None), pl.ds(start, extent)
+
+    def outer(self, flow, core, side):
+        first, extent = flow[0](side), flow[1]
+        if self.along == "rows":
+            return pl.ds(pl.multiple_of(core * self.half_rows + first, 16), extent), slice(None)
+        if self.along == "columns":
+            return slice(None), pl.ds(
+                pl.multiple_of(core * self.half_columns + first, 128), extent
+            )
+        return slice(None), slice(None)
+
+    def extent(self, flow):
+        if self.along == "rows":
+            return flow[1], self.half_columns
+        return self.half_rows, flow[1]
+
+
+SPOTS = [(1, 3), (-1, 3), (1, 2), (-1, 2), (1, 1), (-1, 1), (1, 0)]
+
+
+def reduce_scratch(parts):
+    shapes = []
+    for part in parts:
+        half = (LINE * PAIR, part.half_rows, part.half_columns)
+        shapes.append(pltpu.VMEM(half, part.dtype))
+        shapes.append(pltpu.VMEM(half if part.along else half[1:], part.dtype))
+        for flow in part.flows:
+            rows, columns = part.extent(flow)
+            shapes.append(
+                pltpu.VMEM((LINE * PAIR if flow[3] else 1, rows, columns), part.dtype)
+            )
+            shapes.append(
+                pltpu.VMEM((LINE if flow[2] == "line" else 1, rows, columns), part.dtype)
+            )
+            shapes.append(
+                pltpu.VMEM(
+                    ((LINE + 1) * (1 if flow[2] == "line" else PAIR), rows, columns), part.dtype
+                )
+            )
+    return shapes
+
+
+def reduce_labels(parts):
+    labels = Labels()
+    for n, part in enumerate(parts):
+        for way, steps in SPOTS:
+            for other in (False, True):
+                labels((n, "twin", way, steps, other))
+        labels((n, "twinend"))
+        for k, flow in enumerate(part.flows):
+            for way, steps in SPOTS:
+                for other in (False, True):
+                    if flow[3]:
+                        labels((n, k, "side", way, steps, other))
+                    if flow[2] == "pair" or not other:
+                        labels((n, k, "line", way, steps, other))
+                        if steps == 0:
+                            labels((n, k, "line", -way, steps, other))
+                if flow[2] == "line" or steps == 0:
+                    labels((n, k, "pair", way, steps))
+            labels((n, k, "sideend"))
+            labels((n, k, "twinend"))
+            labels((n, k, "twinsideend"))
+    return labels
+
+
+class Reduce:
+    def __init__(self, place, parts, grads, outs, scratch, send, recv, load):
+        self.place, self.parts, self.grads, self.outs = place, parts, grads, outs
+        self.send, self.recv, self.load = send, recv, load
+        self.labels = reduce_labels(parts)
+        self.sent = []
+        self.own, self.other, self.lanes = [], [], []
+        at = 0
+        for part in parts:
+            self.own.append(scratch[at])
+            self.other.append(scratch[at + 1])
+            at += 2
+            lanes = []
+            for _ in part.flows:
+                lanes.append(scratch[at : at + 3])
+                at += 3
+            self.lanes.append(lanes)
+
+    def copy(self, source, target, key, peer):
+        label = self.labels(key)
+        return pltpu.make_async_remote_copy(
+            source,
+            target,
+            self.send.at[label],
+            self.recv.at[label],
+            device_id=peer,
+            device_id_type=MESH,
+        )
+
+    def start(self, conditions, copy):
+        when(conditions, copy.start)
+        self.sent.append((conditions, copy))
+
+    def there(self, spot):
+        return self.place.has(-spot[0], spot[1])
+
+    def shard(self, spot, other):
+        return self.place.shard_of(-spot[0], spot[1], other)
+
+    def keep(self, n, spot, other):
+        shard = self.shard(spot, other)
+        label = SPOTS.index(spot) * 2 + int(other)
+        return pltpu.make_async_copy(
+            self.parts[n].half(self.grads[n], shard, self.place.core),
+            self.own[n].at[shard],
+            self.load.at[n * 2 * len(SPOTS) + label],
+        )
+
+    def twin(self, n, spot, other, core):
+        shard = self.shard(spot, other)
+        return self.copy(
+            self.parts[n].half(self.grads[n], shard, core),
+            self.other[n].at[shard],
+            (n, "twin") + spot + (other,),
+            self.place.twin(),
+        )
+
+    def begin(self, n):
+        for spot in SPOTS:
+            for other in (True, False):
+                there = self.there(spot)
+                when([there], self.keep(n, spot, other).start)
+                if self.parts[n].along:
+                    self.start([there], self.twin(n, spot, other, 1 - self.place.core))
+
+    def piece(self, n, k, shard, side):
+        part = self.parts[n]
+        rows, columns = part.inner(part.flows[k], side)
+        return self.own[n].at[shard, rows, columns]
+
+    def side_copy(self, n, k, spot, other, side):
+        shard = self.shard(spot, other)
+        return self.copy(
+            self.piece(n, k, shard, side),
+            self.lanes[n][k][0].at[shard],
+            (n, k, "side") + spot + (other,),
+            self.place.beside(),
+        )
+
+    def stage_cores(self, spot):
+        there = self.there(spot)
+        for n, part in enumerate(self.parts):
+            for other in (True, False):
+                shard = self.shard(spot, other)
+
+                def add(n=n, part=part, other=other, shard=shard):
+                    self.keep(n, spot, other).wait()
+                    if part.along:
+                        self.twin(n, spot, other, self.place.core).wait_recv()
+                        self.own[n][shard] = self.own[n][shard] + self.other[n][shard]
+
+                when([there], add)
+        for n, part in enumerate(self.parts):
+            for other in (True, False):
+                for k, flow in enumerate(part.flows):
+                    if flow[3]:
+                        self.start(
+                            [there], self.side_copy(n, k, spot, other, 1 - self.place.side)
+                        )
+
+    def pair_copy(self, n, k, spot, shard):
+        flow = self.parts[n].flows[k]
+        slot = self.place.line + spot[0] * spot[1] if flow[2] == "line" else 0
+        return self.copy(
+            self.piece(n, k, shard, self.place.side),
+            self.lanes[n][k][1].at[slot],
+            (n, k, "pair") + spot,
+            self.place.across(),
+        )
+
+    def stage_sides(self, spot):
+        there = self.there(spot)
+        side = self.place.side
+        for n, part in enumerate(self.parts):
+            for k, flow in enumerate(part.flows):
+                if not flow[3]:
+                    continue
+                for other in (True, False):
+                    shard = self.shard(spot, other)
+
+                    def add(n=n, k=k, other=other, shard=shard):
+                        self.side_copy(n, k, spot, other, side).wait_recv()
+                        piece = self.piece(n, k, shard, side)
+                        piece[...] = piece[...] + self.lanes[n][k][0][shard]
+
+                    when([there], add)
+        for n, part in enumerate(self.parts):
+            for k, flow in enumerate(part.flows):
+                if flow[2] == "line":
+                    self.start([there], self.pair_copy(n, k, spot, self.shard(spot, True)))
+
+    def line_slot(self, flow, way, steps, other, line):
+        slot = line if (steps > 0 or way > 0) else LINE
+        return slot + (LINE + 1) * int(other) if flow[2] == "pair" else slot
+
+    def line_copy(self, n, k, spot, other, arriving):
+        flow = self.parts[n].flows[k]
+        way, steps = spot
+        shard = self.shard(spot, other)
+        line = self.place.line + way * steps
+        left = steps if arriving else steps - 1
+        return self.copy(
+            self.piece(n, k, shard, self.place.side),
+            self.lanes[n][k][2].at[self.line_slot(flow, way, left, other, line)],
+            (n, k, "line", way, left, other),
+            self.place.ahead(way),
+        )
+
+    def stage_line(self, spot):
+        place = self.place
+        there = self.there(spot)
+        way, steps = spot
+        side = place.side
+        todo = []
+        for n, part in enumerate(self.parts):
+            for k, flow in enumerate(part.flows):
+                if flow[2] == "line":
+                    shard = self.shard(spot, False)
+
+                    def add(n=n, k=k, shard=shard):
+                        self.pair_copy(n, k, spot, shard).wait_recv()
+                        slot = place.line + way * steps
+                        piece = self.piece(n, k, shard, side)
+                        piece[...] = piece[...] + self.lanes[n][k][1][slot]
+
+                    when([there], add)
+                for other in (True, False) if flow[2] == "pair" else (False,):
+                    for direction in (1, -1) if steps == 0 else (way,):
+                        here = (direction, steps)
+
+                        def add_line(n=n, k=k, other=other, here=here, flow=flow):
+                            self.line_copy(n, k, here, other, True).wait_recv()
+                            shard = self.shard(here, other)
+                            piece = self.piece(n, k, shard, side)
+                            slot = self.line_slot(
+                                flow, here[0], here[1], other, place.line + here[0] * here[1]
+                            )
+                            piece[...] = piece[...] + self.lanes[n][k][2][slot]
+
+                        when([there, place.can(-direction)], add_line)
+                    if steps > 0:
+                        todo.append(
+                            lambda n=n, k=k, other=other: self.start(
+                                [there], self.line_copy(n, k, spot, other, False)
+                            )
+                        )
+        for action in todo:
+            action()
+
+    def out_view(self, n, k, core, side):
+        part = self.parts[n]
+        rows, columns = part.outer(part.flows[k], core, side)
+        return self.outs[n].at[rows, columns]
+
+    def out_copy(self, n, k, key, peer, core, side):
+        view = self.out_view(n, k, core, side)
+        return self.copy(view, view, (n, k, key), peer)
+
+    def last(self):
+        place = self.place
+        core, side = place.core, place.side
+        spot = (1, 0)
+        here = place.shard
+        everything = [(n, k) for n, part in enumerate(self.parts) for k in range(len(part.flows))]
+        for n, k in everything:
+            if self.parts[n].flows[k][2] == "pair":
+                self.start([], self.pair_copy(n, k, spot, self.shard(spot, True)))
+        for n, k in everything:
+            if self.parts[n].flows[k][2] == "pair":
+                self.pair_copy(n, k, spot, here).wait_recv()
+                piece = self.piece(n, k, here, side)
+                piece[...] = piece[...] + self.lanes[n][k][1][0]
+
+        def swap(n, k):
+            return self.copy(
+                self.piece(n, k, here, side),
+                self.lanes[n][k][0].at[0],
+                (n, k, "sideend"),
+                place.beside(),
+            )
+
+        for n, k in everything:
+            if not self.parts[n].flows[k][3]:
+                self.start([], swap(n, k))
+        for n, k in everything:
+            if self.parts[n].flows[k][3]:
+                self.out_view(n, k, core, side)[...] = self.piece(n, k, here, side)[...]
+        for n, k in everything:
+            if self.parts[n].flows[k][3]:
+                self.start([], self.out_copy(n, k, "sideend", place.beside(), core, side))
+                self.start([], self.out_copy(n, k, "twinend", place.twin(), core, side))
+        for n, k in everything:
+            if not self.parts[n].flows[k][3]:
+                swap(n, k).wait_recv()
+                self.out_view(n, k, core, side)[...] = (
+                    self.piece(n, k, here, side)[...] + self.lanes[n][k][0][0]
+                )
+        for n, k in everything:
+            if not self.parts[n].flows[k][3] and self.parts[n].along:
+                self.start([], self.out_copy(n, k, "twinend", place.twin(), core, side))
+        for n, k in everything:
+            if not self.parts[n].along:
+                self.start([], self.whole(n, k))
+        for n, k in everything:
+            if self.parts[n].flows[k][3]:
+                self.out_copy(n, k, "sideend", place.beside(), core, 1 - side).wait_recv()
+                self.start([], self.out_copy(n, k, "twinsideend", place.twin(), core, 1 - side))
+        for n, k in everything:
+            if self.parts[n].along:
+                self.out_copy(n, k, "twinend", place.twin(), 1 - core, side).wait_recv()
+                if self.parts[n].flows[k][3]:
+                    self.out_copy(
+                        n, k, "twinsideend", place.twin(), 1 - core, 1 - side
+                    ).wait_recv()
+            else:
+                self.whole(n, k).wait_recv()
+        for conditions, copy in self.sent:
+            when(conditions, copy.wait_send)
+        for n, k in everything:
+            if not self.parts[n].along:
+                view = self.out_view(n, k, core, side)
+                view[...] = view[...] + self.other[n][...]
+
+    def whole(self, n, k):
+        return self.copy(
+            self.out_view(n, k, self.place.core, self.place.side),
+            self.other[n],
+            (n, k, "twinend"),
+            self.place.twin(),
+        )
+
+    def steps(self):
+        todo = [lambda n=n: self.begin(n) for n in range(len(self.parts))]
+        for tick in range(len(SPOTS) + 2):
+            if tick < len(SPOTS):
+                todo.append(lambda spot=SPOTS[tick]: self.stage_cores(spot))
+            if 0 <= tick - 1 < len(SPOTS):
+                todo.append(lambda spot=SPOTS[tick - 1]: self.stage_sides(spot))
+            if 0 <= tick - 2 < len(SPOTS):
+                todo.append(lambda spot=SPOTS[tick - 2]: self.stage_line(spot))
+        todo.append(self.last)
+        return todo
+
+
+def reduce_kernel(parts, *refs):
+    count = len(parts)
+    grads, outs = refs[:count], refs[count : 2 * count]
+    scratch, (send, recv, load) = refs[2 * count : -3], refs[-3:]
+    place = Place()
+    greet(place)
+    work = Reduce(place, parts, grads, outs, scratch, send, recv, load)
+    for step in work.steps():
+        step()
+
+
+def reduce_call(arrays, parts, collective_id):
+    labels = reduce_labels(parts)
+    count = len(arrays)
+    return pl.pallas_call(
+        functools.partial(reduce_kernel, parts),
+        out_shape=[jax.ShapeDtypeStruct((p.rows, p.columns), p.dtype) for p in parts],
+        in_specs=[pl.BlockSpec(memory_space=pl.ANY)] * count,
+        out_specs=[pl.BlockSpec(memory_space=pltpu.VMEM)] * count,
+        scratch_shapes=reduce_scratch(parts)
+        + [
+            pltpu.SemaphoreType.DMA((len(labels.numbers),)),
+            pltpu.SemaphoreType.DMA((len(labels.numbers),)),
+            pltpu.SemaphoreType.DMA((count * 2 * len(SPOTS),)),
+        ],
+        compiler_params=pltpu.CompilerParams(
+            collective_id=collective_id, has_side_effects=True, vmem_limit_bytes=63 << 20
+        ),
+        name="reduce_gradients",
+    )(*arrays)
+
+
+def column_part(rows, columns, shared, early):
+    half = columns // 2
+    part = (half - shared) // 2
+    flows = []
+    if shared:
+        flows.append((lambda side: 0, shared, "line", False))
+    if early:
+        flows.append((lambda side: shared + side * part, early, "line", True))
+    if part > early:
+        flows.append((lambda side: shared + side * part + early, part - early, "pair", True))
+    return Part(rows, columns, "columns", flows)
+
+
+def row_part(rows, columns, shared, early):
+    half = rows // 2
+    part = (half - shared) // 2
+    return Part(
+        rows,
+        columns,
+        "rows",
+        [
+            (lambda side: 0, shared, "line", False),
+            (lambda side: shared + side * part, early, "line", True),
+            (lambda side: shared + side * part + early, part - early, "pair", True),
+        ],
+    )
+
+
+def vector_part(rows, columns):
+    return Part(rows, columns, None, [(lambda side: 0, columns, "line", False)], F32)
 
 
 def exact_gelu(hidden):
@@ -96,6 +896,82 @@
         (key_part * scale).astype(BF16).reshape(keys_all.shape),
         value_part.astype(BF16).reshape(values_all.shape),
     )
+
+
+def direct(width):
+    return lax.axis_size("fsdp") == LINE * PAIR and lax.axis_size("ctx") == 4 and width % 1024 == 0
+
+
+def gather_all(vectors, qkv, output, inner, outer):
+    arrays = (qkv, output, inner, outer)
+    if not direct(output.shape[1]):
+        return (lax.all_gather(vectors, "fsdp", axis=0, tiled=False),) + tuple(
+            gather_rows(part) for part in arrays
+        )
+    shards = lax.axis_size("fsdp")
+    lanes = 128
+    rows = -(-vectors.shape[0] // (16 * lanes)) * 16
+    table = jnp.pad(vectors, (0, rows * lanes - vectors.shape[0])).reshape(rows, lanes)
+    flows = [Flow(0, rows, lambda core, side: (0, rows, 0, lanes), cores=False)]
+    flows += gather_columns(1, qkv)
+    flows += gather_columns(2, output)
+    flows += gather_columns(3, inner)
+    flows += gather_lines(4, outer)
+    full = gather_call((table,) + arrays, flows, shards, 1)
+    packed = full[0].reshape(shards, rows * lanes)[:, : vectors.shape[0]]
+    return (packed,) + tuple(full[1:])
+
+
+def near(value, share, unit):
+    return int(round(value * share / unit)) * unit
+
+
+def gather_columns(number, shard):
+    rows, columns = shard.shape
+    half = columns // 2
+    shared = half - 2 * near(half, 0.32, 128)
+    return column_flows(number, rows, columns, shared, max(128, near(half - shared, 0.3, 128)))
+
+
+def gather_lines(number, shard):
+    rows, columns = shard.shape
+    half = rows // 2
+    shared = half - 2 * near(half, 0.32, 16)
+    return row_flows(number, rows, columns, shared, near(half - shared, 0.3, 16))
+
+
+def reduce_columns(rows, columns):
+    half = columns // 2
+    shared = half - 2 * near(half, 0.25, 128)
+    return column_part(rows, columns, shared, near(half - shared, 0.25, 128))
+
+
+def reduce_lines(rows, columns):
+    half = rows // 2
+    shared = half - 2 * near(half, 0.25, 16)
+    return row_part(rows, columns, shared, near(half - shared, 0.25, 16))
+
+
+def reduce_all(vectors, qkv, output, inner, outer):
+    shards, count = vectors.shape
+    if not direct(output.shape[1]):
+        share = lax.psum_scatter(vectors, "fsdp", scatter_dimension=0, tiled=True)
+        return (lax.psum(share, "ctx")[0],) + tuple(
+            reduce_rows(part) for part in (qkv, output, inner, outer)
+        )
+    lanes = 128
+    rows = -(-count // (16 * lanes)) * 16
+    table = jnp.pad(vectors, ((0, 0), (0, rows * lanes - count))).reshape(shards * rows, lanes)
+    parts = [
+        reduce_columns(inner.shape[0] // shards, inner.shape[1]),
+        reduce_lines(outer.shape[0] // shards, outer.shape[1]),
+        reduce_columns(output.shape[0] // shards, output.shape[1]),
+        reduce_columns(qkv.shape[0] // shards, qkv.shape[1]),
+        vector_part(rows, lanes),
+    ]
+    sums = reduce_call((inner, outer, output, qkv, table), parts, 2)
+    share = sums[4].reshape(-1)[:count]
+    return (share, sums[3].astype(F32), sums[2].astype(F32), sums[0].astype(F32), sums[1].astype(F32))
 
 
 def gather_rows(part):
@@ -139,7 +1015,13 @@
         second_shift,
     )
     widths = [member.shape[0] for member in vectors]
-    packed = lax.all_gather(jnp.concatenate(vectors), "fsdp", axis=0, tiled=False)
+    packed, full_qkv, full_output, full_inner, full_outer = gather_all(
+        jnp.concatenate(vectors),
+        jnp.concatenate((query_weight, key_weight, value_weight), axis=1),
+        output_weight,
+        inner_weight,
+        outer_weight,
+    )
     (
         bias_query,
         bias_value,
@@ -151,11 +1033,6 @@
         gain_second,
         shift_second,
     ) = [piece.reshape(-1).astype(F32) for piece in split_columns(packed, widths)]
-    full_qkv = gather_rows(jnp.concatenate((query_weight, key_weight, value_weight), axis=1))
-    full_output = gather_rows(output_weight)
-    full_inner = gather_rows(inner_weight)
-    full_outer = gather_rows(outer_weight)
-
     micro, seqs, block_len, width = inputs.shape
     heads = width // HEAD_DIM
     ctx_size = lax.axis_size("ctx")
@@ -224,10 +1101,6 @@
     value_bias_part = column_sums(qkv_grad[:, 2 * width :])
     input_grad = first_grad + right_product(qkv_grad, full_qkv)
 
-    qkv_share = reduce_rows(qkv_weight_part)
-    output_share = reduce_rows(output_weight_part)
-    inner_share = reduce_rows(inner_weight_part)
-    outer_share = reduce_rows(outer_weight_part)
     vector_parts = (
         query_bias_part,
         value_bias_part,
@@ -243,9 +1116,9 @@
     packed_parts = jnp.concatenate(
         [part.reshape(fsdp_size, -1) for part in vector_parts], axis=1
     )
-    vector_share = lax.psum(
-        lax.psum_scatter(packed_parts, "fsdp", scatter_dimension=0, tiled=True), "ctx"
-    )[0]
+    vector_share, qkv_share, output_share, inner_share, outer_share = reduce_all(
+        packed_parts, qkv_weight_part, output_weight_part, inner_weight_part, outer_weight_part
+    )
     shares = split_columns(vector_share, widths)
     query_share, key_share, value_share = split_columns(qkv_share, [width] * 3)
     return (

time: 1160 us -> 564 us (0.49)
  waiting for transfers between devices: 882 us -> 49.2 us
  Pallas kernels: 0 us -> 326 us
  blocking collectives: 67.2 us -> 0 us
  local copies, waits for them, and re-layouts: 63 us -> 48.3 us
    reduce_scatter x3 -> x0, waiting for transfers between devices: 374 us -> none  [reduce_rows(): lax.psum_scatter(part.astype(BF16), 'fsdp', scatter_dimension=0, tiled=True)]
    pallas_call x0 -> x2, Pallas kernels: none -> 326 us  [the longest x1 200 us: reduce_call(): pl.pallas_call(functools.partial(reduce_kernel, parts), out_shape=[jax.Sh...]
    all_gather x4 -> x0, waiting for transfers between devices: 325 us -> none  [gather_rows(): return lax.all_gather(part, 'fsdp', axis=0, tiled=True)]
    unnamed x12 -> x2, waiting for transfers between devices: 98.3 us -> 0.03 us
    unnamed x1 -> x0, blocking collectives: 28.6 us -> none
    all_gather x1 -> x0, blocking collectives: 25.8 us -> none  [body(): lax.all_gather(jnp.concatenate(vectors), 'fsdp', axis=0, tiled=False)]
    psum x1 -> x0, waiting for transfers between devices: 22 us -> none  [reduce_rows(): return lax.psum(share, 'ctx').astype(F32)]
    unnamed x70 -> x77, local copies, waits for them, and re-layouts: 31.4 us -> 12.3 us
  transfers between devices with their start and end apart: 11 -> 2, of which waited for: 11 -> 2; matrix products, arithmetic and copies ran while one was open for 8% -> 4% of each run, Pallas kernels for 0% -> 0%
where the time goes in v2:
time: 564 us; the launch traced here: 555 us
  Pallas kernels  326 us (58%)
  matrix products  88.5 us (16%)
  waiting for transfers between devices  49.2 us (9%)
  local copies, waits for them, and re-layouts  48.3 us (9%)
  other arithmetic  27.8 us (5%)
  between operations  15 us (3%)
    pallas_call x1, Pallas kernels, reduce_call(): pl.pallas_call(functools.partial(reduce_kernel, parts), out_shape=[jax.Sh...  200 us
    pallas_call x1, Pallas kernels, gather_call(): pl.pallas_call(functools.partial(gather_kernel, flows, count), out_shape=...  126 us
    all_gather x1, waiting for transfers between devices, body(): lax.all_gather(keys_values.reshape(group, block_len, 2 * width), 'ctx', a...  27.8 us
    dot_general x4, matrix products, right_product(): lax.dot_general(left, right, (((1,), (1,)), ((), ())), preferred_element_...  25.8 us
    reduce_scatter x1, waiting for transfers between devices, body(): lax.psum_scatter(jnp.concatenate((key_part, value_part), axis=2), 'ctx',...  21.4 us
    dot_general x4, matrix products, plain_product(): return jnp.dot(left, right, preferred_element_type=F32)  21.2 us
    dot_general x4, matrix products, left_product(): lax.dot_general(left, right, (((0,), (0,)), ((), ())), preferred_element_...  17.9 us
    unnamed x77, local copies, waits for them, and re-layouts  12.3 us
  transfers between devices with their start and end apart: 2, of which 2 were waited for; matrix products, arithmetic and copies ran while one was open for 4% of the time, Pallas kernels for 0%

profile of v2, /device:TPU:1, one launch (start us, length us, event | category | flops | bytes accessed | tf_op | source)
XLA Modules:
  0.0 555.2 jit_solution(8797407044550097965)
XLA Ops:
  15.4 2.0 pad_maximum_fusion.5.refs_1_
  17.5 126.4 %gather_weights.1 = (bf16[128,128]{1,0:T(8,128)(2,1)}, bf16[1024,3072]{1,0:T(8,128)(2,1)}, bf16[1024,1024]{1,0:T(8,128)(2,1)}, bf16[1024,4096]{1,0:T(8,128)(2,1)}, bf16[4096,1024]{1,0:T(8,128)(2,1)}) custom-call(bf16[16,128]{1,0:T(8,128)(2,1)} %pad_bitcast_fusion.refs_0_, bf16[128,3072]{1,0:T(8,128)(2,1)} %pad_maximum_fusion.5.refs_1_, ...), custom_call_target="tpu_custom_call" | custom-call | tf_op jit(solution)/shard_map/gather_weights/pallas_call | solution.py:301
  144.6 4.6 convolution_bitcast_fusion
  153.7 27.8 %all-gather.2.cloned.1.call-done = bf16[2,512,2048]{2,1,0:T(8,128)(2,1)} async-done(((bf16[2,128,2048]{2,1,0:T(8,128)(2,1)}), bf16[2,512,2048]{2,1,0:T(8,128)(2,1)}) %all-gather.2.cloned.1.call-update) | async-done | bytes 4194320 | tf_op jit(solution)/shard_map/all_gather | solution.py:1053
  181.6 4.2 fusion.52
  185.8 2.5 copy.46
  188.3 2.9 copy.44
  191.2 7.6 %fusion.54 = (f32[2,16,128]{2,1,0:T(8,128)S(1)}, f32[2,16,128,512]{3,2,1,0:T(8,128)}) fusion(pred[2,512]{1,0:T(4,128)(4,1)S(1)} %iota_compare_fusion, bf16[2,128,16,64]{1,3,2,0:T(8,128)(2,1)S(1)} %copy-done.21, bf16[2,512,16,64]{1,3,2,0:T(8,128)(2,1)} %bitcast.164), kind=kOutput, calls=%fused_computation.146 | convolution fusion | flops 276824576 | bytes 11027456 | tf_op jit(solution)/shard_map/sub | solution.py:868
  198.8 4.0 divide_convert_fusion
  207.7 13.3 %multiply_convert_fusion.1 = (bf16[256,4096]{1,0:T(8,128)(2,1)S(1)}, f32[256,4096]{1,0:T(8,128)S(1)}, f32[256,4096]{1,0:T(8,128)}) fusion(f32[4096]{0:T(1024)S(1)} %bitcast.177, bf16[1024,4096]{1,0:T(8,128)(2,1)S(1)} %bitcast.181, f32[256,1024]{1,0:T(8,128)S(1)} %get-tuple-element.114, f32[1024]{0:T(1024)S(1)} %get-tuple-element.96, ...), kind=kOutput, calls=%fused_computation.19 | convolution fusion | flops 2218000384 | bytes 19949568 | tf_op jit(solution)/shard_map/dot_general | solution.py:817
  221.1 2.5 fusion.56
  225.6 11.4 %convert_reduce_fusion = (f32[4096]{0:T(1024)S(1)}, bf16[256,4096]{1,0:T(8,128)(2,1)S(1)}) fusion(f32[256,4096]{1,0:T(8,128)S(1)} %get-tuple-element.84, f32[256,4096]{1,0:T(8,128)} %get-tuple-element.115, bf16[4096,1024]{1,0:T(8,128)(2,1)} %get-tuple-element.31, f32[256,1024]{1,0:T(8,128)S(1)} %get-tuple-element.80), kind=kOutput, calls=%fused_computation.16 | convolution fusion | flops 2164518912 | bytes 19939328 | tf_op jit(solution)/shard_map/dot_general | solution.py:825
  237.0 6.8 %multiply_reduce_fusion.1 = (f32[1024]{0:T(1024)S(1)}, f32[256]{0:T(256)S(1)}, f32[256]{0:T(256)S(1)}, f32[1024]{0:T(1024)S(1)}, f32[256,1024]{1,0:T(8,128)S(1)}) fusion(f32[256,1024]{1,0:T(8,128)S(1)} %get-tuple-element.114, f32[256]{0:T(256)S(1)} %add_rsqrt_fusion.1, f32[256]{0:T(256)S(1)} %broadcast_multiply_fusion.4, f32[1024]{0:T(1024)S(1)} %get-tuple-element.97, ...), kind=kOutput, calls=%fused_computation.61 | convolution fusion | flops 2150102528 | bytes 13647872 | tf_op jit(solution)/shard_map/dot_general | solution.py:825
  246.8 2.5 reshape.336
  249.3 2.8 copy.50
  252.0 4.5 convolution_convert_fusion.2
  256.6 4.7 fusion.1
  261.3 3.9 copy.55
  265.2 6.5 %fusion.2 = bf16[2,16,128,512]{3,2,1,0:T(8,128)(2,1)S(1)} fusion(f32[2,16,128,512]{3,2,1,0:T(8,128)} %get-tuple-element.120, f32[2,16,128]{2,1,0:T(8,128)S(1)} %get-tuple-element.119, f32[2,16,128,512]{3,2,1,0:T(8,128)} %get-tuple-element.112, f32[2,16,128]{2,1,0:T(8,128)S(1)} %get-tuple-element.111), kind=kLoop, calls=%fused_computation.4 | loop fusion | flops 12582912 | bytes 21004288 | tf_op jit(solution)/shard_map/convert_element_type | solution.py:886
  271.8 2.0 copy-done.2
  274.4 2.4 copy.54
  276.8 4.7 pad_maximum_fusion
  281.6 4.5 convert_reduce_fusion.4
  287.9 2.2 reshape.334
  290.1 2.0 convolution_convert_fusion.3.refs_2_
  293.0 5.6 %convolution_convert_fusion.refs_1_ = bf16[4096,1024]{1,0:T(8,128)(2,1)} fusion(bf16[256,4096]{1,0:T(8,128)(2,1)S(1)} %copy-done.14, f32[256,1024]{1,0:T(8,128)S(1)} %copy-done.12), kind=kOutput, calls=%fused_computation.8 | convolution fusion | flops 2151940096 | bytes 11534336 | tf_op jit(solution)/shard_map/dot_general | solution.py:821
  298.7 5.7 %convolution_convert_fusion.1.refs_0_ = bf16[1024,4096]{1,0:T(8,128)(2,1)} fusion(bf16[256,4096]{1,0:T(8,128)(2,1)S(1)} %copy-done.17, f32[256,1024]{1,0:T(8,128)S(1)} %get-tuple-element.114, f32[1024]{0:T(1024)S(1)} %get-tuple-element.96, f32[1024]{0:T(1024)S(1)} %get-tuple-element.97, f32[256]{0:T(256)S(1)} %add_rsqrt_fusion.1, ...), kind=kOutput, calls=%fused_computation.9 | convolution fusion | flops 2152988672 | bytes 11544576 | tf_op jit(solution)/shard_map/dot_general | solution.py:821
  304.4 21.4 %reduce-scatter.2.cloned.1.call-done = bf16[2,128,2048]{2,1,0:T(8,128)(2,1)} async-done(((bf16[2,512,2048]{2,1,0:T(8,128)(2,1)}), bf16[2,128,2048]{2,1,0:T(8,128)(2,1)}) %reduce-scatter.2.cloned.1.call-update) | async-done | bytes 1048592 | tf_op jit(solution)/shard_map/reduce_scatter | solution.py:1095
  326.9 6.0 %convolution_add_fusion.2 = f32[256,1024]{1,0:T(8,128)} fusion(f32[256,1024]{1,0:T(8,128)S(1)} %copy-done.4, bf16[1024,3072]{1,0:T(8,128)(2,1)} %get-tuple-element.27, bf16[256,2048]{1,0:T(8,128)(2,1)} %bitcast.169, bf16[256,1024]{1,0:T(8,128)(2,1)S(1)} %reshape.334), kind=kOutput, calls=%fused_computation.43 | convolution fusion | flops 1614020608 | bytes 9961472 | tf_op jit(solution)/shard_map/dot_general | solution.py:825
  332.9 4.5 convert_bitcast_fusion.refs_3_
  338.1 199.7 %reduce_gradients.1 = (bf16[128,4096]{1,0:T(8,128)(2,1)}, bf16[512,1024]{1,0:T(8,128)(2,1)}, bf16[128,1024]{1,0:T(8,128)(2,1)}, bf16[128,3072]{1,0:T(8,128)(2,1)}, f32[16,128]{1,0:T(8,128)}) custom-call(bf16[1024,4096]{1,0:T(8,128)(2,1)} %convolution_convert_fusion.1.refs_0_, bf16[4096,1024]{1,0:T(8,128)(2,1)} %convolution_convert_fusion.refs_1_, ...), custom_call_target="tpu_custom_call" | custom-call | tf_op jit(solution)/shard_map/reduce_gradients/pallas_call | solution.py:762
  542.5 2.3 fusion.53
  (126 shorter events, 36.2 us)
Async XLA Ops:
  7.2 137.5 %copy-start.18 = (bf16[2,1,128,1024]{3,2,1,0:T(8,128)(2,1)S(1)}, bf16[2,1,128,1024]{3,2,1,0:T(8,128)(2,1)}, u32[]{:S(2)}) copy-start(bf16[2,1,128,1024]{3,2,1,0:T(8,128)(2,1)} %param.18) | copy-start | bytes 1572868
  7.2 174.4 %all-gather.2.cloned.1.call-start = ((), (), s32[]{:S(2)}) async-start(), calls=%async_computation.1 | async-start | bytes 5242880 | tf_op jit(solution)/shard_map/all_gather | solution.py:1053
  149.3 3.9 copy-start.25
  149.3 4.0 copy-start.8
  150.7 175.1 %reduce-scatter.2.cloned.1.call-start = ((), (), s32[]{:S(2)}) async-start(), calls=%async_computation.2 | async-start | bytes 5242880 | tf_op jit(solution)/shard_map/reduce_scatter | solution.py:1095
  188.3 2.9 copy-start.21
  198.8 8.5 %slice-start = ((s8[8388608]{0:T(1024)(128)(4,1)}), s8[4194304]{0:T(1024)(128)(4,1)S(1)}, s32[]{:S(2)}) async-start(s8[8388608]{0:T(1024)(128)(4,1)} %bitcast.180), calls=%async_computation.3 | async-start | bytes 8388608
  202.8 4.2 copy-start
  202.9 3.1 copy-start.5
  202.9 3.4 copy-start.19
  202.9 4.8 slice-start.1
  205.0 16.0 %copy-start.6 = (bf16[2,128,16,64]{1,0,3,2:T(2,128)(2,1)}, bf16[2,128,16,64]{1,0,3,2:T(2,128)(2,1)S(1)}, u32[]{:S(2)}) copy-start(bf16[2,128,16,64]{1,0,3,2:T(2,128)(2,1)S(1)} %copy.48) | copy-start | bytes 1572868
  206.2 14.8 %slice-start.2 = ((s8[8388608]{0:T(1024)(128)(4,1)}), s8[4194304]{0:T(1024)(128)(4,1)S(1)}, s32[]{:S(2)}) async-start(s8[8388608]{0:T(1024)(128)(4,1)} %bitcast.182), calls=%async_computation.5 | async-start | bytes 8388608
  207.7 13.3 %slice-start.3 = ((s8[8388608]{0:T(1024)(128)(4,1)}), s8[4194304]{0:T(1024)(128)(4,1)S(1)}, s32[]{:S(2)}) async-start(s8[8388608]{0:T(1024)(128)(4,1)} %bitcast.182), calls=%async_computation.6 | async-start | bytes 8388608
  221.0 2.5 copy-start.13
  221.0 2.8 copy-start.9
  225.6 11.4 %copy-start.11 = (f32[256,1024]{1,0:T(8,128)}, f32[256,1024]{1,0:T(8,128)S(1)}, u32[]{:S(2)}) copy-start(f32[256,1024]{1,0:T(8,128)S(1)} %get-tuple-element.80) | copy-start | bytes 3145732
  237.0 6.9 %copy-start.16 = (bf16[256,4096]{1,0:T(8,128)(2,1)}, bf16[256,4096]{1,0:T(8,128)(2,1)S(1)}, u32[]{:S(2)}) copy-start(bf16[256,4096]{1,0:T(8,128)(2,1)S(1)} %get-tuple-element.124) | copy-start | bytes 6291460
  244.3 1.0 copy-start.3
  252.0 4.5 copy-start.1
  252.0 4.5 copy-start.10
  265.2 8.5 %copy-start.22 = (bf16[2,128,16,64]{1,3,2,0:T(8,128)(2,1)S(1)}, bf16[2,128,16,64]{1,3,2,0:T(8,128)(2,1)}, u32[]{:S(2)}) copy-start(bf16[2,128,16,64]{1,3,2,0:T(8,128)(2,1)} %copy.47) | copy-start | bytes 1572868
  271.8 2.0 copy-start.2
  281.5 8.5 %copy-start.4 = (f32[256,1024]{1,0:T(8,128)S(1)}, f32[256,1024]{1,0:T(8,128)}, u32[]{:S(2)}) copy-start(f32[256,1024]{1,0:T(8,128)} %copy-done.3) | copy-start | bytes 3145732
  281.5 8.5 %copy-start.7 = (bf16[2,128,16,64]{1,0,3,2:T(2,128)(2,1)S(1)}, bf16[2,128,16,64]{1,0,3,2:T(2,128)(2,1)}, u32[]{:S(2)}) copy-start(bf16[2,128,16,64]{1,0,3,2:T(2,128)(2,1)} %copy-done.6) | copy-start | bytes 1572868
  290.0 2.1 copy-start.12
  290.0 3.0 copy-start.14
  293.0 5.6 %copy-start.17 = (bf16[256,4096]{1,0:T(8,128)(2,1)S(1)}, bf16[256,4096]{1,0:T(8,128)(2,1)}, u32[]{:S(2)}) copy-start(bf16[256,4096]{1,0:T(8,128)(2,1)} %copy-done.16) | copy-start | bytes 6291460
  326.9 6.0 %copy-start.15 = (bf16[2,128,2048]{2,1,0:T(8,128)(2,1)S(1)}, bf16[2,128,2048]{2,1,0:T(8,128)(2,1)}, u32[]{:S(2)}) copy-start(bf16[2,128,2048]{2,1,0:T(8,128)(2,1)} %reduce-scatter.2.cloned.1.call-done) | copy-start | bytes 3145732
  326.9 6.0 %copy-start.20 = (bf16[2,1,128,1024]{3,2,1,0:T(8,128)(2,1)S(1)}, bf16[2,1,128,1024]{3,2,1,0:T(8,128)(2,1)}, u32[]{:S(2)}) copy-start(bf16[2,1,128,1024]{3,2,1,0:T(8,128)(2,1)} %param.18) | copy-start | bytes 1572868
  537.9 6.9 %copy-start.24 = (bf16[128,4096]{1,0:T(8,128)(2,1)S(1)}, bf16[128,4096]{1,0:T(8,128)(2,1)}, u32[]{:S(2)}) copy-start(bf16[128,4096]{1,0:T(8,128)(2,1)} %get-tuple-element.35) | copy-start | bytes 3145732
  537.9 8.5 %copy-start.23 = (bf16[512,1024]{1,0:T(8,128)(2,1)S(1)}, bf16[512,1024]{1,0:T(8,128)(2,1)}, u32[]{:S(2)}) copy-start(bf16[512,1024]{1,0:T(8,128)(2,1)} %get-tuple-element.36) | copy-start | bytes 3145732
Sparse Core Ops, SparseCore 0:
  150.8 30.7 all-gather.1
  281.6 44.0 reduce-scatter.1
